TPU v7x, 32 devices: a whole 2x2x4 slice. The times are simulated.
32 devices in a mesh: dp: 8 (over y, x, core), tensor: 4 (over z).
Axes of the slice: x: 2, y: 2, z: 4, core: 2. Of those that a mesh axis runs over, the one named last changes fastest.
Arguments:
- tokens: bfloat16 [16384, 768], P('dp'), may hold values from -24 to 24
- lengths: int32 [8, 8], P('dp'), may hold values from 1 to 512, 2048 in all within a row
- w_qkv: bfloat16 [3, 768, 768], P(None, None, 'tensor'), may hold values from -0.21875 to 0.21875
- b_qv: bfloat16 [2, 768], P(None, 'tensor'), may hold values from -3 to 3
- w_out: bfloat16 [768, 768], P('tensor'), may hold values from -0.875 to 0.875
- b_out: bfloat16 [768], replicated, may hold values from -3 to 3
- ln1_gain: bfloat16 [768], replicated, may hold values from 0.099609375 to 1.8984375
- ln1_bias: bfloat16 [768], replicated, may hold values from -3 to 3
- w_up: bfloat16 [768, 3072], P(None, 'tensor'), may hold values from -0.21875 to 0.21875
- b_up: bfloat16 [3072], P('tensor'), may hold values from -3 to 3
- w_down: bfloat16 [3072, 768], P('tensor'), may hold values from -0.109375 to 0.109375
- b_down: bfloat16 [768], replicated, may hold values from -3 to 3
- ln2_gain: bfloat16 [768], replicated, may hold values from 0.099609375 to 1.8984375
- ln2_bias: bfloat16 [768], replicated, may hold values from -3 to 3
- cotangent: bfloat16 [16384, 768], P('dp'), may hold values from -24 to 24
Outputs:
- layer_out: bfloat16 [16384, 768], P(('dp', 'tensor'))
- input_grad: bfloat16 [16384, 768], P(('dp', 'tensor'))
- grad_qkv: float32 [3, 768, 768], P(None, 'dp', 'tensor')
- grad_qv_bias: float32 [2, 768], P(None, 'tensor')
- grad_out: float32 [768, 768], P('tensor', 'dp')
- grad_out_bias: float32 [768], P('dp')
- grad_norm1_gain: float32 [768], P('dp')
- grad_norm1_bias: float32 [768], P('dp')
- grad_up: float32 [768, 3072], P('dp', 'tensor')
- grad_up_bias: float32 [3072], P('tensor')
- grad_down: float32 [3072, 768], P('tensor', 'dp')
- grad_down_bias: float32 [768], P('dp')
- grad_norm2_gain: float32 [768], P('dp')
- grad_norm2_bias: float32 [768], P('dp')
Inputs may be any that keep to these rules, and one draw needn't show every extreme that they name: Each row holds 8 lengths that sum to 2048; the longest pair of every pack has exactly 512 tokens.
All inputs are finite; a program needn't handle non-finite values.
Results may differ from a plain program's by a relative error of at most 0.02.
Values may be sent and summed in bfloat16 or wider, within the bound.
A program may use at most 192 MiB of HBM per device.

v0:
```python
import jax
import jax.numpy as jnp
from jax import lax
from jax.sharding import PartitionSpec as P

HD = 64
MOST = 512


epsilon = 1e-05


def segment_ids(pair_lengths, count):
    pair_ends = jnp.cumsum(pair_lengths)
    positions = jnp.arange(count, dtype=jnp.int32)
    return jnp.sum((positions[:, None] >= pair_ends[None, :]).astype(jnp.int32), axis=1)


def norm_forward(values, gain, shift_bias):
    average = jnp.mean(values, axis=-1, keepdims=True)
    centred = values - average
    inv_spread = lax.rsqrt(jnp.mean(centred * centred, axis=-1, keepdims=True) + epsilon)
    normed = centred * inv_spread
    return (normed * gain + shift_bias, normed, inv_spread)


def norm_backward(upstream, normed, inv_spread, gain):
    scaled = upstream * gain
    adjusted = (
        scaled
        - jnp.mean(scaled, axis=-1, keepdims=True)
        - normed * jnp.mean(scaled * normed, axis=-1, keepdims=True)
    )
    return (adjusted * inv_spread, jnp.sum(upstream * normed, axis=0), jnp.sum(upstream, axis=0))


def gelu_exact(value):
    return jax.nn.gelu(value, approximate=False)


def per_device(
    tokens,
    lengths,
    w_qkv,
    b_qv,
    w_out,
    b_out,
    ln1_gain,
    ln1_bias,
    w_up,
    b_up,
    w_down,
    b_down,
    ln2_gain,
    ln2_bias,
    cotangent,
):
    rows = tokens.shape[0]
    local_width = w_out.shape[0]
    local_heads = local_width // HD
    blocks = rows // MOST
    window_rows = 3 * MOST
    factor = HD ** (-0.5)
    segment = segment_ids(lengths[0], rows)
    segment_pad = jnp.pad(segment, (MOST, MOST), constant_values=-1)
    projected = jnp.einsum("td,cde->cte", tokens, w_qkv, preferred_element_type=jnp.float32)
    bias_rows = jnp.stack([b_qv[0], jnp.zeros_like(b_qv[0]), b_qv[1]]).astype(jnp.float32)
    qkv_low = (projected + bias_rows[:, None, :]).astype(jnp.bfloat16)
    padded = jnp.pad(qkv_low[1:], ((0, 0), (MOST, MOST), (0, 0)))

    def block_scores(block_index):
        offset = block_index * MOST
        queries = lax.dynamic_slice_in_dim(qkv_low[0], offset, MOST, 0).reshape(
            MOST, local_heads, HD
        )
        window = lax.dynamic_slice_in_dim(padded, offset, window_rows, 1).reshape(
            2, window_rows, local_heads, HD
        )
        query_segment = lax.dynamic_slice_in_dim(segment, offset, MOST, 0)
        key_segment = lax.dynamic_slice_in_dim(segment_pad, offset, window_rows, 0)
        allowed = query_segment[:, None] == key_segment[None, :]
        products = (
            jnp.einsum("qhd,khd->hqk", queries, window[0], preferred_element_type=jnp.float32)
            * factor
        )
        return (jnp.where(allowed[None], products, -1e30), queries, window)

    def forward_block(block_index):
        scores, queries, window = block_scores(block_index)
        row_top = jnp.max(scores, axis=-1, keepdims=True)
        row_total = jnp.sum(jnp.exp(scores - row_top), axis=-1, keepdims=True)
        log_total = row_top + jnp.log(row_total)
        soft_weights = jnp.exp(scores - log_total).astype(jnp.bfloat16)
        context = jnp.einsum(
            "hqk,khd->qhd", soft_weights, window[1], preferred_element_type=jnp.float32
        )
        return (context.reshape(MOST, local_width).astype(jnp.bfloat16), log_total[..., 0])

    contexts, log_totals = lax.map(forward_block, jnp.arange(blocks, dtype=jnp.int32))
    context = contexts.reshape(rows, local_width)
    attended = lax.psum(
        jnp.dot(context, w_out, preferred_element_type=jnp.float32).astype(jnp.bfloat16), "tensor"
    ).astype(jnp.float32)
    mixed_one = tokens.astype(jnp.float32) + attended + b_out.astype(jnp.float32)
    gain_one = ln1_gain.astype(jnp.float32)
    hidden_one, normed_one, spread_one = norm_forward(
        mixed_one, gain_one, ln1_bias.astype(jnp.float32)
    )
    hidden_low = hidden_one.astype(jnp.bfloat16)
    pre_act = jnp.dot(hidden_low, w_up, preferred_element_type=jnp.float32) + b_up.astype(
        jnp.float32
    )
    activated = gelu_exact(pre_act).astype(jnp.bfloat16)
    fed = lax.psum(
        jnp.dot(activated, w_down, preferred_element_type=jnp.float32).astype(jnp.bfloat16),
        "tensor",
    ).astype(jnp.float32)
    mixed_two = hidden_one + fed + b_down.astype(jnp.float32)
    gain_two = ln2_gain.astype(jnp.float32)
    output_full, normed_two, spread_two = norm_forward(
        mixed_two, gain_two, ln2_bias.astype(jnp.float32)
    )
    share = rows // lax.axis_size("tensor")
    own_start = lax.axis_index("tensor") * share
    layer_out = lax.dynamic_slice_in_dim(output_full, own_start, share, 0).astype(jnp.bfloat16)
    upstream = cotangent.astype(jnp.float32)
    grad_mixed_two, grad_gain_two, grad_bias_two = norm_backward(
        upstream, normed_two, spread_two, gain_two
    )
    grad_fed = grad_mixed_two.astype(jnp.bfloat16)
    grad_down_t = jnp.einsum("td,tf->df", grad_fed, activated, preferred_element_type=jnp.float32)
    grad_act = jnp.einsum("td,fd->tf", grad_fed, w_down, preferred_element_type=jnp.float32)
    act_pull = jax.vjp(gelu_exact, pre_act)[1]
    grad_pre = act_pull(grad_act)[0].astype(jnp.bfloat16)
    grad_up_local = jnp.einsum(
        "td,tf->df", hidden_low, grad_pre, preferred_element_type=jnp.float32
    )
    up_bias_sum = jnp.sum(grad_pre.astype(jnp.float32), axis=0)
    partial_hidden = jnp.einsum("tf,df->td", grad_pre, w_up, preferred_element_type=jnp.float32)
    grad_hidden_one = (
        lax.psum(partial_hidden.astype(jnp.bfloat16), "tensor").astype(jnp.float32) + grad_mixed_two
    )
    grad_mixed_one, grad_gain_one, grad_bias_one = norm_backward(
        grad_hidden_one, normed_one, spread_one, gain_one
    )
    sum_mixed_one = jnp.sum(grad_mixed_one, axis=0)
    grad_attended = grad_mixed_one.astype(jnp.bfloat16)
    own_mixed_one = lax.dynamic_slice_in_dim(grad_mixed_one, own_start, share, 0)
    grad_out_t = jnp.einsum("td,tc->dc", grad_attended, context, preferred_element_type=jnp.float32)
    grad_context = jnp.einsum(
        "td,cd->tc", grad_attended, w_out, preferred_element_type=jnp.float32
    ).astype(jnp.bfloat16)

    def backward_block(gathered_grads, block_index):
        offset = block_index * MOST
        scores, queries, window = block_scores(block_index)
        soft_weights = jnp.exp(scores - log_totals[block_index][..., None])
        upstream_block = lax.dynamic_slice_in_dim(grad_context, offset, MOST, 0).reshape(
            MOST, local_heads, HD
        )
        grad_values = jnp.einsum(
            "hqk,qhd->khd",
            soft_weights.astype(jnp.bfloat16),
            upstream_block,
            preferred_element_type=jnp.float32,
        )
        grad_weights = jnp.einsum(
            "qhd,khd->hqk", upstream_block, window[1], preferred_element_type=jnp.float32
        )
        row_shift = jnp.sum(grad_weights * soft_weights, axis=-1, keepdims=True)
        grad_scores = (soft_weights * (grad_weights - row_shift)).astype(jnp.bfloat16)
        grad_queries = (
            jnp.einsum("hqk,khd->qhd", grad_scores, window[0], preferred_element_type=jnp.float32)
            * factor
        )
        grad_keys = (
            jnp.einsum("hqk,qhd->khd", grad_scores, queries, preferred_element_type=jnp.float32)
            * factor
        )
        update = jnp.stack(
            [
                grad_keys.reshape(window_rows, local_width),
                grad_values.reshape(window_rows, local_width),
            ]
        )
        current = lax.dynamic_slice_in_dim(gathered_grads, offset, window_rows, 1)
        gathered_grads = lax.dynamic_update_slice_in_dim(
            gathered_grads, current + update, offset, 1
        )
        return (gathered_grads, grad_queries.reshape(MOST, local_width))

    start_grads = jnp.zeros((2, rows + 2 * MOST, local_width), jnp.float32)
    key_value_grads, query_grads = lax.scan(
        backward_block, start_grads, jnp.arange(blocks, dtype=jnp.int32)
    )
    key_value_grads = key_value_grads[:, MOST : MOST + rows]
    grad_qkv_low = jnp.stack(
        [query_grads.reshape(rows, local_width), key_value_grads[0], key_value_grads[1]]
    ).astype(jnp.bfloat16)
    grad_qkv_t = jnp.einsum("td,cte->dce", tokens, grad_qkv_low, preferred_element_type=jnp.float32)
    qkv_bias_sums = jnp.sum(grad_qkv_low.astype(jnp.float32), axis=1)
    partial_input = jnp.einsum(
        "cte,cde->td", grad_qkv_low, w_qkv, preferred_element_type=jnp.float32
    )
    input_share = lax.psum_scatter(
        partial_input.astype(jnp.bfloat16), "tensor", scatter_dimension=0, tiled=True
    ).astype(jnp.float32)
    input_grad = (input_share + own_mixed_one).astype(jnp.bfloat16)
    bias_grads, up_bias_grad = lax.psum(
        (jnp.stack([qkv_bias_sums[0], qkv_bias_sums[2]]), up_bias_sum), "dp"
    )
    small_stack = jnp.stack(
        [
            sum_mixed_one,
            grad_gain_one,
            grad_bias_one,
            jnp.sum(grad_mixed_two, axis=0),
            grad_gain_two,
            grad_bias_two,
        ],
        axis=1,
    )
    qkv_share, out_share, small_share, up_share, down_share = (
        lax.psum_scatter(grad_qkv_t, "dp", scatter_dimension=0, tiled=True),
        lax.psum_scatter(grad_out_t, "dp", scatter_dimension=0, tiled=True),
        lax.psum_scatter(small_stack, "dp", scatter_dimension=0, tiled=True),
        lax.psum_scatter(grad_up_local, "dp", scatter_dimension=0, tiled=True),
        lax.psum_scatter(grad_down_t, "dp", scatter_dimension=0, tiled=True),
    )
    return (
        layer_out,
        input_grad,
        jnp.transpose(qkv_share, (1, 0, 2)),
        bias_grads,
        out_share.T,
        small_share[:, 0],
        small_share[:, 1],
        small_share[:, 2],
        up_share,
        up_bias_grad,
        down_share.T,
        small_share[:, 3],
        small_share[:, 4],
        small_share[:, 5],
    )


def solution(mesh):
    return jax.shard_map(
        per_device,
        mesh=mesh,
        in_specs=(
            P("dp", None),
            P("dp", None),
            P(None, None, "tensor"),
            P(None, "tensor"),
            P("tensor", None),
            P(),
            P(),
            P(),
            P(None, "tensor"),
            P("tensor"),
            P("tensor", None),
            P(),
            P(),
            P(),
            P("dp", None),
        ),
        out_specs=(
            P(("dp", "tensor"), None),
            P(("dp", "tensor"), None),
            P(None, "dp", "tensor"),
            P(None, "tensor"),
            P("tensor", "dp"),
            P("dp"),
            P("dp"),
            P("dp"),
            P("dp", "tensor"),
            P("tensor"),
            P("tensor", "dp"),
            P("dp"),
            P("dp"),
            P("dp"),
        ),
        check_vma=False,
    )
```

profile of v0, /device:TPU:0, one launch (start us, length us, event | category | flops | bytes accessed | tf_op | source)
XLA Modules:
  0.0 892.9 jit_solution(6782802428937616471)
XLA Ops:
  9.8 4.2 fusion.30
  15.4 51.2 %while.24 = (s32[]{:T(128)}, bf16[4,512,192]{1,2,0:T(8,128)(2,1)}, f32[4,3,512]{2,1,0:T(4,128)}, s32[4]{0:T(128)S(1)}, bf16[2,3072,192]{1,2,0:T(8,128)(2,1)S(1)}...) while((s32[]{:T(128)}, bf16[4,512,192]{1,2,0:T(8,128)(2,1)}, ...), condition=%wide.region_5.6_spmd, body=%wide.region_2.5_spmd.sunk | while | flops 630815232 | bytes 37824776 | solution.py:99
  21.3 2.8 exponential_reduce_fusion.2
  34.1 2.8 exponential_reduce_fusion.2
  46.9 2.8 exponential_reduce_fusion.2
  59.7 2.8 exponential_reduce_fusion.2
  68.7 3.7 convolution_convert_fusion.2
  77.1 119.2 %all-reduce.7.cloned.1.call-done = bf16[2048,768]{1,0:T(8,128)(2,1)} async-done(((bf16[2048,768]{1,0:T(8,128)(2,1)}), bf16[2048,768]{1,0:T(8,128)(2,1)}) %all-reduce.7.cloned.1.call-update) | async-done | bytes 3145744 | tf_op jit(solution)/shard_map/psum | solution.py:101
  196.3 4.1 fusion.23
  202.9 18.6 %multiply_convert_fusion.1 = (bf16[2048,768]{1,0:T(8,128)(2,1)S(1)}, f32[2048,768]{1,0:T(8,128)}, f32[2048,768]{1,0:T(8,128)}) fusion(f32[768]{0:T(1024)S(1)} %copy-done.42, bf16[768,768]{1,0:T(8,128)(2,1)S(1)} %copy-done, f32[768]{0:T(1024)S(1)} %copy-done.38, f32[768]{0:T(1024)S(1)} %copy-done.34, f32[2048]{0:T(1024)S(1)} %add_rsqrt_fusion.1, ...), kind=kOutput, calls=%fused_computation.53 | convolution fusion | flops 2533883904 | bytes 23228416 | tf_op jit(solution)/shard_map/dot_general | solution.py:110
  223.1 4.0 convolution_convert_fusion.1
  229.9 117.4 %all-reduce.9.cloned.1.call-done = bf16[2048,768]{1,0:T(8,128)(2,1)} async-done(((bf16[2048,768]{1,0:T(8,128)(2,1)}), bf16[2048,768]{1,0:T(8,128)(2,1)}) %all-reduce.9.cloned.1.call-update) | async-done | bytes 3145744 | tf_op jit(solution)/shard_map/psum | solution.py:114
  347.3 6.5 fusion.48
  353.9 3.9 multiply_reduce_fusion.3
  357.9 6.5 fusion.16
  367.0 10.4 %convert_reduce_fusion.1 = (f32[768]{0:T(1024)}, bf16[2048,768]{1,0:T(8,128)(2,1)S(1)}) fusion(f32[2048,768]{1,0:T(8,128)} %get-tuple-element.223, bf16[768,768]{1,0:T(8,128)(2,1)S(1)} %copy-done.45, f32[2048,768]{1,0:T(8,128)S(1)} %fusion.13, f32[2048,768]{1,0:T(8,128)} %get-tuple-element.242, f32[768]{0:T(1024)S(1)} %copy-done.43), kind=kOutput, calls=%fused_computation.45 | convolution fusion | flops 2444229888 | bytes 23205888 | tf_op jit(solution)/shard_map/td,fd->tf/dot_general | solution.py:132
  379.0 4.0 convolution_convert_fusion
  385.0 118.3 %all-reduce.11.cloned.1.call-done = bf16[2048,768]{1,0:T(8,128)(2,1)} async-done(((bf16[2048,768]{1,0:T(8,128)(2,1)}), bf16[2048,768]{1,0:T(8,128)(2,1)}) %all-reduce.11.cloned.1.call-update) | async-done | bytes 3145744 | tf_op jit(solution)/shard_map/psum | solution.py:141
  503.3 7.9 multiply_reduce_fusion.1
  511.6 5.7 fusion.52
  523.0 4.8 convolution_convert_fusion.3
  528.1 2.8 broadcast_in_dim.42
  530.9 148.0 %while.25 = (s32[]{:T(128)}, f32[2,3072,192]{1,2,0:T(8,128)}, bf16[4,512,192]{1,2,0:T(8,128)(2,1)}, s32[4]{0:T(128)S(1)}, bf16[3,2048,192]{1,2,0:T(8,128)(2,1)},...) while((s32[]{:T(128)}, f32[2,3072,192]{1,2,0:T(8,128)}, ...), condition=%wide.region_19.20_spmd, body=%wide.region_17.19_spmd.sunk | while | flops 1533639168 | bytes 149576176 | solution.py:193
  542.7 5.6 multiply_reduce_fusion.7
  548.2 9.4 %multiply_convert_fusion.3 = bf16[3,512,1536]{2,1,0:T(8,128)(2,1)} fusion(f32[3,512,1536]{2,1,0:T(8,128)} %copy-done.2, f32[3,512,1536]{2,1,0:T(8,128)} %get-tuple-element.375, f32[3,512]{1,0:T(4,128)S(1)} %get-tuple-element.376), kind=kLoop, calls=%fused_computation.16.clone.1 | loop fusion | flops 7077888 | bytes 23599104 | tf_op jit(solution)/shard_map/while/body/eval_jaxpr/convert_element_type | solution.py:171
  557.7 4.2 convolution_multiply_fusion.5
  564.4 3.5 fusion.116
  579.7 5.6 multiply_reduce_fusion.7
  585.3 9.5 %multiply_convert_fusion.3 = bf16[3,512,1536]{2,1,0:T(8,128)(2,1)} fusion(f32[3,512,1536]{2,1,0:T(8,128)} %copy-done.2, f32[3,512,1536]{2,1,0:T(8,128)} %get-tuple-element.375, f32[3,512]{1,0:T(4,128)S(1)} %get-tuple-element.376), kind=kLoop, calls=%fused_computation.16.clone.1 | loop fusion | flops 7077888 | bytes 23599104 | tf_op jit(solution)/shard_map/while/body/eval_jaxpr/convert_element_type | solution.py:171
  594.8 4.2 convolution_multiply_fusion.5
  601.6 3.5 fusion.116
  616.8 5.5 multiply_reduce_fusion.7
  622.3 9.4 %multiply_convert_fusion.3 = bf16[3,512,1536]{2,1,0:T(8,128)(2,1)} fusion(f32[3,512,1536]{2,1,0:T(8,128)} %copy-done.2, f32[3,512,1536]{2,1,0:T(8,128)} %get-tuple-element.375, f32[3,512]{1,0:T(4,128)S(1)} %get-tuple-element.376), kind=kLoop, calls=%fused_computation.16.clone.1 | loop fusion | flops 7077888 | bytes 23599104 | tf_op jit(solution)/shard_map/while/body/eval_jaxpr/convert_element_type | solution.py:171
  631.7 4.2 convolution_multiply_fusion.5
  638.5 3.5 fusion.116
  653.7 5.5 multiply_reduce_fusion.7
  659.3 9.4 %multiply_convert_fusion.3 = bf16[3,512,1536]{2,1,0:T(8,128)(2,1)} fusion(f32[3,512,1536]{2,1,0:T(8,128)} %copy-done.2, f32[3,512,1536]{2,1,0:T(8,128)} %get-tuple-element.375, f32[3,512]{1,0:T(4,128)S(1)} %get-tuple-element.376), kind=kLoop, calls=%fused_computation.16.clone.1 | loop fusion | flops 7077888 | bytes 23599104 | tf_op jit(solution)/shard_map/while/body/eval_jaxpr/convert_element_type | solution.py:171
  668.7 4.2 convolution_multiply_fusion.5
  675.4 3.5 fusion.116
  683.4 5.2 fusion.24
  688.6 2.8 copy.48
  691.7 4.1 bitcast_convert_fusion
  695.8 8.2 fusion.38
  704.1 8.6 fusion.44
  716.3 14.7 %all-reduce.2 = (f32[2,192]{1,0:T(2,128)}, f32[768]{0:T(1024)}) all-reduce(f32[2,192]{1,0:T(2,128)S(1)} %pad_maximum_fusion.3, f32[768]{0:T(1024)S(1)} %copy-done.41), channel_id=1, replica_groups=mesh['dp'=8,'tensor'=4] {'dp'}, use_global_device_ids=true, to_apply=%region_23.24 | all-reduce | flops 1152 | bytes 9216 | tf_op jit(solution)/shard_map/psum | solution.py:209
  739.3 54.3 %reduce-scatter.11.cloned.1.call-done = bf16[512,768]{1,0:T(8,128)(2,1)} async-done(((bf16[2048,768]{1,0:T(8,128)(2,1)}), bf16[512,768]{1,0:T(8,128)(2,1)}) %reduce-scatter.11.cloned.1.call-update) | async-done | bytes 786448 | tf_op jit(solution)/shard_map/reduce_scatter | solution.py:205
  796.3 43.6 %reduce-scatter.17.cloned.1.call-done = f32[96,768]{1,0:T(8,128)} async-done(((f32[768,768]{1,0:T(8,128)}), f32[96,768]{1,0:T(8,128)}) %reduce-scatter.17.cloned.1.call-update) | async-done | bytes 294928 | tf_op jit(solution)/shard_map/reduce_scatter | solution.py:228
  839.8 46.3 %reduce-scatter.15.cloned.1.call-done = f32[96,768]{1,0:T(8,128)} async-done(((f32[768,768]{1,0:T(8,128)}), f32[96,768]{1,0:T(8,128)}) %reduce-scatter.15.cloned.1.call-update) | async-done | bytes 294928 | tf_op jit(solution)/shard_map/reduce_scatter | solution.py:227
  (306 shorter events, 133.0 us)
Async XLA Ops:
  7.2 195.6 %copy-start = (bf16[768,768]{1,0:T(8,128)(2,1)S(1)}, bf16[768,768]{1,0:T(8,128)(2,1)}, u32[]{:S(2)}) copy-start(bf16[768,768]{1,0:T(8,128)(2,1)} %param.27) | copy-start | bytes 3538948
  7.2 189.1 %all-reduce.7.cloned.1.call-start = ((), (), s32[]{:S(2)}) async-start(), calls=%async_computation.6 | async-start | bytes 6291456 | tf_op jit(solution)/shard_map/psum | solution.py:101
  72.4 274.9 %all-reduce.9.cloned.1.call-start = ((), (), s32[]{:S(2)}) async-start(), calls=%async_computation.7 | async-start | bytes 6291456 | tf_op jit(solution)/shard_map/psum | solution.py:114
  73.3 437.9 %copy-start.33 = (f32[768]{0:T(1024)}, f32[768]{0:T(1024)S(1)}, u32[]{:S(2)}) copy-start(f32[768]{0:T(1024)S(1)} %convert_element_type.132) | copy-start | bytes 9220
  196.3 6.5 copy-start.34
  196.3 6.5 copy-start.38
  196.3 6.5 copy-start.42
  201.0 20.5 %copy-start.25 = (f32[2048]{0:T(1024)}, f32[2048]{0:T(1024)S(1)}, u32[]{:S(2)}) copy-start(f32[2048]{0:T(1024)S(1)} %broadcast_multiply_fusion.5) | copy-start | bytes 24580
  202.8 18.6 %copy-start.29 = (f32[2048]{0:T(1024)}, f32[2048]{0:T(1024)S(1)}, u32[]{:S(2)}) copy-start(f32[2048]{0:T(1024)S(1)} %add_rsqrt_fusion.1) | copy-start | bytes 24580
  202.8 20.2 %copy-start.44 = (bf16[768,768]{1,0:T(8,128)(2,1)S(1)}, bf16[768,768]{1,0:T(8,128)(2,1)}, u32[]{:S(2)}) copy-start(bf16[768,768]{1,0:T(8,128)(2,1)} %param.29) | copy-start | bytes 3538948
  227.1 276.2 %all-reduce.11.cloned.1.call-start = ((), (), s32[]{:S(2)}) async-start(), calls=%async_computation.8 | async-start | bytes 6291456 | tf_op jit(solution)/shard_map/psum | solution.py:141
  347.3 6.6 copy-start.5
  347.3 6.6 copy-start.8
  347.3 6.6 copy-start.15
  347.3 6.6 copy-start.26
  347.3 6.6 copy-start.30
  347.3 6.6 copy-start.35
  347.3 6.6 copy-start.39
  347.3 6.6 copy-start.40
  367.0 10.4 %copy-start.10 = (f32[2048,768]{1,0:T(8,128)}, f32[2048,768]{1,0:T(8,128)S(1)}, u32[]{:S(2)}) copy-start(f32[2048,768]{1,0:T(8,128)S(1)} %fusion.13) | copy-start | bytes 18874372
  383.1 347.9 %reduce-scatter.21.cloned.1.call-start = ((), (), s32[]{:S(2)}) async-start(), calls=%async_computation.14 | async-start | bytes 442368
  385.0 126.3 %copy-start.27 = (f32[2048]{0:T(1024)S(1)}, f32[2048]{0:T(1024)}, u32[]{:S(2)}) copy-start(f32[2048]{0:T(1024)} %copy-done.25) | copy-start | bytes 24580
  385.0 126.3 %copy-start.31 = (f32[2048]{0:T(1024)S(1)}, f32[2048]{0:T(1024)}, u32[]{:S(2)}) copy-start(f32[2048]{0:T(1024)} %copy-done.29) | copy-start | bytes 24580
  385.0 126.3 %copy-start.36 = (f32[768]{0:T(1024)S(1)}, f32[768]{0:T(1024)}, u32[]{:S(2)}) copy-start(f32[768]{0:T(1024)} %convert_element_type.133) | copy-start | bytes 9220
  503.3 8.0 copy-start.6
  503.3 8.0 copy-start.9
  503.3 8.3 copy-start.18
  511.6 8.4 copy-start.20
  523.0 212.7 %reduce-scatter.13.cloned.1.call-start = ((), (), s32[]{:S(2)}) async-start(), calls=%async_computation.10 | async-start | bytes 884736 | tf_op jit(solution)/shard_map/reduce_scatter | solution.py:225
  527.9 209.5 %reduce-scatter.19.cloned.1.call-start = ((), (), s32[]{:S(2)}) async-start(), calls=%async_computation.13 | async-start | bytes 2211840
  530.9 10.8 %copy-start.23 = (s32[3072]{0:T(1024)}, s32[3072]{0:T(1024)S(1)}, u32[]{:S(2)}) copy-start(s32[3072]{0:T(1024)S(1)} %get-tuple-element.459) | copy-start | bytes 36868 | tf_op jit(solution)/shard_map/while
  541.7 6.5 copy-start.2
  561.9 6.1 copy-start.24
  568.0 10.8 %copy-start.23 = (s32[3072]{0:T(1024)}, s32[3072]{0:T(1024)S(1)}, u32[]{:S(2)}) copy-start(s32[3072]{0:T(1024)S(1)} %get-tuple-element.459) | copy-start | bytes 36868 | tf_op jit(solution)/shard_map/while
  578.8 6.6 copy-start.2
  605.0 10.8 %copy-start.23 = (s32[3072]{0:T(1024)}, s32[3072]{0:T(1024)S(1)}, u32[]{:S(2)}) copy-start(s32[3072]{0:T(1024)S(1)} %get-tuple-element.459) | copy-start | bytes 36868 | tf_op jit(solution)/shard_map/while
  615.9 6.5 copy-start.2
  635.9 6.0 copy-start.24
  642.0 10.8 %copy-start.23 = (s32[3072]{0:T(1024)}, s32[3072]{0:T(1024)S(1)}, u32[]{:S(2)}) copy-start(s32[3072]{0:T(1024)S(1)} %get-tuple-element.459) | copy-start | bytes 36868 | tf_op jit(solution)/shard_map/while
  652.8 6.5 copy-start.2
  672.9 6.0 copy-start.24
  683.4 8.3 copy-start.46
  691.4 102.3 %reduce-scatter.11.cloned.1.call-start = ((), (), s32[]{:S(2)}) async-start(), calls=%async_computation.9 | async-start | bytes 3932160 | tf_op jit(solution)/shard_map/reduce_scatter | solution.py:205
  695.7 8.3 copy-start.28
  695.8 8.3 copy-start.32
  695.8 144.1 %reduce-scatter.17.cloned.1.call-start = ((), (), s32[]{:S(2)}) async-start(), calls=%async_computation.12 | async-start | bytes 2654208 | tf_op jit(solution)/shard_map/reduce_scatter | solution.py:228
  704.0 182.1 %reduce-scatter.15.cloned.1.call-start = ((), (), s32[]{:S(2)}) async-start(), calls=%async_computation.11 | async-start | bytes 2654208 | tf_op jit(solution)/shard_map/reduce_scatter | solution.py:227
  704.1 182.1 %copy-start.1 = (bf16[768,768]{1,0:T(8,128)(2,1)S(1)}, bf16[768,768]{1,0:T(8,128)(2,1)}, u32[]{:S(2)}) copy-start(bf16[768,768]{1,0:T(8,128)(2,1)} %param.27) | copy-start | bytes 3538948
  (27 other events, 71.0 us)
Sparse Core Ops, SparseCore 0:
  72.5 123.7 all-reduce.6
  227.2 120.0 all-reduce.8
  383.2 120.0 all-reduce.10
  523.1 32.8 reduce-scatter.20
  559.0 34.9 reduce-scatter.12
  691.5 39.3 reduce-scatter.18
  733.2 60.4 reduce-scatter.10
  797.6 42.2 reduce-scatter.16
  843.8 42.3 reduce-scatter.14
where the time goes:
time: 901 us; the launch traced here: 893 us
  waiting for transfers between devices  499 us (55%)
  matrix products  156 us (17%)
  other arithmetic  122 us (14%)
  local copies, waits for them, and re-layouts  70.2 us (8%)
  blocking collectives  14.7 us (2%)
  between operations  14.7 us (2%)
  loops' own time  13.6 us (2%)
    psum x1, waiting for transfers between devices, per_device(): lax.psum(jnp.dot(context, w_out, preferred_element_type=jnp.float32).asty...  119 us
    psum x1, waiting for transfers between devices, per_device(): lax.psum(partial_hidden.astype(jnp.bfloat16), 'tensor').astype(jnp.float32)  118 us
    psum x1, waiting for transfers between devices, per_device(): lax.psum(jnp.dot(activated, w_down, preferred_element_type=jnp.float32).a...  117 us
    reduce_scatter x1, waiting for transfers between devices, per_device(): lax.psum_scatter(partial_input.astype(jnp.bfloat16), 'tensor', scatter_di...  54.3 us
    reduce_scatter x1, waiting for transfers between devices, per_device(): lax.psum_scatter(grad_up_local, 'dp', scatter_dimension=0, tiled=True)  46.3 us
    reduce_scatter x1, waiting for transfers between devices, per_device(): lax.psum_scatter(grad_down_t, 'dp', scatter_dimension=0, tiled=True)  43.6 us
    convert_element_type x4, other arithmetic, backward_block(): (soft_weights * (grad_weights - row_shift)).astype(jnp.bfloat16)  37.7 us
    dot_general x4, matrix products, backward_block(): jnp.einsum('qhd,khd->hqk', upstream_block, window[1], preferred_element_t...  22.2 us
  transfers between devices with their start and end apart: 9, of which 6 were waited for; matrix products, arithmetic and copies ran while one was open for 22% of the time, Pallas kernels for 0%

commit v1 on v0

v1 whole, which is shorter than its diff:
```python
import functools

import jax
import jax.numpy as jnp
from jax import lax
from jax.experimental import pallas as pl
from jax.experimental.pallas import tpu as pltpu
from jax.sharding import PartitionSpec as P

HD = 64
MOST = 512
GROUP = 8
TILE = 256
epsilon = 1e-05
MESH = pl.DeviceIdType.MESH
F32 = jnp.float32
BF16 = jnp.bfloat16


def mm(a, b):
    return lax.dot_general(a, b, (((1,), (0,)), ((), ())), preferred_element_type=F32)


def mm_nt(a, b):
    return lax.dot_general(a, b, (((1,), (1,)), ((), ())), preferred_element_type=F32)


def mm_tn(a, b):
    return lax.dot_general(a, b, (((0,), (0,)), ((), ())), preferred_element_type=F32)


def mm_tt(a, b):
    return lax.dot_general(a, b, (((0,), (1,)), ((), ())), preferred_element_type=F32)


def peers_of(group_rank):
    core = group_rank % 2
    along_x = (group_rank // 2) % 2
    along_y = group_rank // 4
    step_x = 2 - 4 * along_x
    step_y = 4 - 8 * along_y
    return group_rank + 1 - 2 * core, group_rank + step_x, group_rank + step_y, group_rank + step_x + step_y


def greet(devices):
    barrier = pltpu.get_barrier_semaphore()
    for device in devices:
        pl.semaphore_signal(barrier, inc=1, device_id=device, device_id_type=MESH)
    pl.semaphore_wait(barrier, len(devices))


def remote(src, dst, send_sem, recv_sem, device):
    return pltpu.make_async_remote_copy(
        src_ref=src, dst_ref=dst, send_sem=send_sem, recv_sem=recv_sem, device_id=device, device_id_type=MESH
    )


def forward_kernel(
    parts, tok, wqkv, bias, seg_row, seg_col, up, down, out,
    q_t, k_n, v_t, lse, ctx_all, up_all, down_all, out_all,
    k_pad, v_pad, ctx, z_send, z_recv, x_send, x_recv, c_send, c_recv, a_send, a_recv, l_sem,
):
    rows = tok.shape[0]
    width = wqkv.shape[2]
    heads = width // HD
    share = rows // parts
    dp = lax.axis_index("dp")
    me = lax.axis_index("tensor")
    rank = dp % GROUP
    base = dp - rank
    others = peers_of(rank)
    shards = (out, up, down)
    fulls = (out_all, up_all, down_all)

    def at(j):
        return (me + j) % parts

    greet([(dp, at(j)) for j in range(1, parts)] + [(base + other, me) for other in others])

    def z_copy(w, j):
        return remote(
            shards[w].at[rank], fulls[w].at[me, rank], z_send.at[w, j - 1], z_recv.at[w, j - 1], (dp, at(j))
        )

    def x_copy(w, j, k, slot):
        source = at(parts - j)
        piece = fulls[w].at[source, slot]
        return remote(piece, piece, x_send.at[w, j - 1, k], x_recv.at[w, j - 1, k], (base + others[1 + k], me))

    def c_copy(w, j, k, slot):
        source = at(parts - j)
        piece = fulls[w].at[source, slot]
        return remote(piece, piece, c_send.at[w, j - 1, k], c_recv.at[w, j - 1, k], (base + others[0], me))

    for w in range(3):
        for j in range(1, parts):
            z_copy(w, j).start()
    own = [pltpu.make_async_copy(shards[w], fulls[w].at[me], l_sem.at[w]) for w in range(3)]
    for copy in own:
        copy.start()

    def spread(w):
        for j in range(1, parts):
            z_copy(w, j).wait_recv()
            for k in range(3):
                x_copy(w, j, k, rank).start()

    def pass_on(w):
        for j in range(1, parts):
            c_copy(w, j, 0, rank).start()
            for k in range(3):
                x_copy(w, j, k, others[1 + k]).wait_recv()
                c_copy(w, j, 1 + k, others[1 + k]).start()

    k_pad[:, :MOST] = jnp.zeros((heads, MOST, HD), BF16)
    k_pad[:, MOST + rows :] = jnp.zeros((heads, MOST, HD), BF16)
    v_pad[:, :MOST] = jnp.zeros((width, MOST), BF16)
    v_pad[:, MOST + rows :] = jnp.zeros((width, MOST), BF16)

    @pl.loop(0, rows // TILE)
    def _(t):
        here = pl.ds(pl.multiple_of(t * TILE, TILE), TILE)
        there = pl.ds(pl.multiple_of(t * TILE + MOST, TILE), TILE)
        x = tok[here, :]
        q_t[:, here] = (mm_tt(wqkv[0], x) + bias[0]).astype(BF16)
        keys = mm(x, wqkv[1]).astype(BF16)
        k_n[here, :] = keys
        for h in range(heads):
            k_pad[h, there, :] = keys[:, h * HD : (h + 1) * HD]
        values = (mm_tt(wqkv[2], x) + bias[1]).astype(BF16)
        v_t[:, here] = values
        v_pad[:, there] = values

    spread(0)
    span = TILE + 2 * MOST
    per_block = share // TILE
    scale = HD ** (-0.5)

    def a_copy(j):
        block = at(j)
        return remote(ctx.at[block], ctx_all.at[me], a_send.at[j - 1], a_recv.at[j - 1], (dp, block))

    @pl.loop(0, rows // TILE)
    def _(step):
        block = (me + 1 + step // per_block) % parts
        inner = (step % per_block) * TILE
        begin = block * share + inner
        here = pl.ds(pl.multiple_of(begin, TILE), TILE)
        window = pl.ds(pl.multiple_of(begin, TILE), span)
        allowed_q = seg_row[:, here]
        allowed_k = seg_col[window, :]
        allowed = jnp.concatenate(
            [allowed_k == allowed_q[:, i * 128 : (i + 1) * 128] for i in range(TILE // 128)], axis=1
        )
        outs = []
        for h in range(heads):
            hs = pl.ds(h * HD, HD)
            queries = q_t[hs, here] * jnp.asarray(scale, BF16)
            scores = jnp.where(allowed, mm(k_pad[h, window, :], queries), -1e30)
            top = jnp.max(scores, axis=0, keepdims=True)
            weights = jnp.exp(scores - top)
            total = jnp.sum(weights, axis=0, keepdims=True)
            lse[h : h + 1, here] = top + jnp.log(total)
            outs.append(mm(v_pad[hs, window], weights.astype(BF16)) / total)
        result = jnp.concatenate(outs, axis=0).T.astype(BF16)
        ctx[block, pl.ds(pl.multiple_of(inner, TILE), TILE), :] = result
        for j in range(1, parts):

            @pl.when(step == j * per_block)
            def _(j=j):
                a_copy(j).start()

        @pl.when(step == 3)
        def _():
            spread(1)

    keep = pltpu.make_async_copy(ctx.at[me], ctx_all.at[me], l_sem.at[3])
    keep.start()
    spread(2)
    for w in range(3):
        pass_on(w)
    for j in range(1, parts):
        a_copy(j).wait()
    for w in range(3):
        for j in range(1, parts):
            z_copy(w, j).wait_send()
            c_copy(w, j, 0, rank).wait_send()
            c_copy(w, j, 0, others[0]).wait_recv()
            for k in range(3):
                x_copy(w, j, k, rank).wait_send()
                c_copy(w, j, 1 + k, others[1 + k]).wait()
    for copy in own:
        copy.wait()
    keep.wait()


def forward_part(parts, tokens, w_qkv, bias, seg_row, seg_col, w_up, w_down, w_out):
    rows, model = tokens.shape
    width = w_qkv.shape[2]
    heads = width // HD
    share = rows // parts

    def sliced(w):
        return w.reshape(GROUP, w.shape[0] // GROUP, w.shape[1])

    shards = [sliced(w) for w in (w_up, w_down, w_out)]
    vmem = pl.BlockSpec(memory_space=pltpu.VMEM)
    hbm = pl.BlockSpec(memory_space=pl.ANY)
    dma = pltpu.SemaphoreType.DMA
    outs = pl.pallas_call(
        functools.partial(forward_kernel, parts),
        out_shape=[
            jax.ShapeDtypeStruct((width, rows), BF16),
            jax.ShapeDtypeStruct((rows, width), BF16),
            jax.ShapeDtypeStruct((width, rows), BF16),
            jax.ShapeDtypeStruct((heads, rows), F32),
            jax.ShapeDtypeStruct((parts, share, width), BF16),
        ]
        + [jax.ShapeDtypeStruct((parts,) + s.shape, BF16) for s in shards],
        in_specs=[vmem] * 8,
        out_specs=[vmem] * 5 + [hbm] * 3,
        scratch_shapes=[
            pltpu.VMEM((heads, rows + 2 * MOST, HD), BF16),
            pltpu.VMEM((width, rows + 2 * MOST), BF16),
            pltpu.VMEM((parts, share, width), BF16),
            dma((3, parts - 1)),
            dma((3, parts - 1)),
            dma((3, parts - 1, 3)),
            dma((3, parts - 1, 3)),
            dma((3, parts - 1, 4)),
            dma((3, parts - 1, 4)),
            dma((parts - 1,)),
            dma((parts - 1,)),
            dma((4,)),
        ],
        compiler_params=pltpu.CompilerParams(
            collective_id=0, has_side_effects=True, vmem_limit_bytes=60 * 1024 * 1024
        ),
        name="forward_part",
    )(tokens, w_qkv, bias, seg_row, seg_col, *shards)
    q_t, k_n, v_t, lse, ctx_all, up_all, down_all, out_all = outs
    return (
        q_t, k_n, v_t, lse, ctx_all,
        up_all.reshape((parts,) + w_up.shape),
        down_all.reshape((parts,) + w_down.shape),
        out_all.reshape((parts,) + w_out.shape),
    )


def segment_ids(pair_lengths, count):
    pair_ends = jnp.cumsum(pair_lengths)
    positions = jnp.arange(count, dtype=jnp.int32)
    return jnp.sum((positions[:, None] >= pair_ends[None, :]).astype(jnp.int32), axis=1)


def norm_forward(values, gain, shift_bias):
    average = jnp.mean(values, axis=-1, keepdims=True)
    centred = values - average
    inv_spread = lax.rsqrt(jnp.mean(centred * centred, axis=-1, keepdims=True) + epsilon)
    normed = centred * inv_spread
    return (normed * gain + shift_bias, normed, inv_spread)


def norm_backward(upstream, normed, inv_spread, gain):
    scaled = upstream * gain
    adjusted = (
        scaled
        - jnp.mean(scaled, axis=-1, keepdims=True)
        - normed * jnp.mean(scaled * normed, axis=-1, keepdims=True)
    )
    return (adjusted * inv_spread, jnp.sum(upstream * normed, axis=0), jnp.sum(upstream, axis=0))


def gelu_exact(value):
    return jax.nn.gelu(value, approximate=False)


def middle_part(parts, x_own, g_own, ctx_all, w_out, w_up, w_down, b_out, g1, s1, b_up, b_down, g2, s2):
    own, width = ctx_all.shape[1], ctx_all.shape[2]
    model = w_out.shape[2]
    ctx = jnp.transpose(ctx_all, (1, 0, 2)).reshape(own, parts * width)
    out_full = w_out.reshape(parts * width, model)
    mixed_one = x_own + mm(ctx, out_full) + b_out
    hidden_one, normed_one, spread_one = norm_forward(mixed_one, g1, s1)
    low = hidden_one.astype(BF16)
    pre = [mm(low, w_up[n]) + b_up[n] for n in range(parts)]
    act = [gelu_exact(p).astype(BF16) for p in pre]
    fed = sum(mm(act[n], w_down[n]) for n in range(parts))
    mixed_two = hidden_one + fed + b_down
    layer_out, normed_two, spread_two = norm_forward(mixed_two, g2, s2)
    grad_two, gain_two, shift_two = norm_backward(g_own, normed_two, spread_two, g2)
    d_fed = grad_two.astype(BF16)
    grad_down = [mm_tn(d_fed, act[n]) for n in range(parts)]
    d_pre = [jax.vjp(gelu_exact, pre[n])[1](mm_nt(d_fed, w_down[n]))[0].astype(BF16) for n in range(parts)]
    grad_up = [mm_tn(low, d_pre[n]) for n in range(parts)]
    up_bias = jnp.stack([jnp.sum(d.astype(F32), axis=0) for d in d_pre])
    grad_hidden = grad_two + sum(mm_nt(d_pre[n], w_up[n]) for n in range(parts))
    grad_one, gain_one, shift_one = norm_backward(grad_hidden, normed_one, spread_one, g1)
    d_att = grad_one.astype(BF16)
    grad_out = [mm_tn(d_att, ctx_all[n]) for n in range(parts)]
    d_ctx = jnp.stack([mm_nt(d_att, w_out[n]).astype(BF16) for n in range(parts)])
    small = jnp.stack(
        [jnp.sum(grad_one, axis=0), gain_one, shift_one, jnp.sum(grad_two, axis=0), gain_two, shift_two]
    )
    return layer_out.astype(BF16), grad_one, d_ctx, grad_down, grad_up, grad_out, up_bias, small


def per_device(
    tokens,
    lengths,
    w_qkv,
    b_qv,
    w_out,
    b_out,
    ln1_gain,
    ln1_bias,
    w_up,
    b_up,
    w_down,
    b_down,
    ln2_gain,
    ln2_bias,
    cotangent,
):
    rows = tokens.shape[0]
    width = w_out.shape[0]
    heads = width // HD
    parts = lax.axis_size("tensor")
    share = rows // parts
    me = lax.axis_index("tensor")
    segment = segment_ids(lengths[0], rows)
    seg_row = segment[None, :]
    seg_col = jnp.broadcast_to(
        jnp.pad(segment, (MOST, MOST), constant_values=-1)[:, None], (rows + 2 * MOST, 128)
    )
    bias = b_qv.astype(F32)[:, :, None]
    q_t, k_n, v_t, lse, ctx_all, up_full, down_full, out_full = forward_part(
        parts, tokens, w_qkv, bias, seg_row, seg_col, w_up, w_down, w_out
    )
    b_up_full = lax.all_gather(b_up, "tensor").astype(F32)
    x_own = lax.dynamic_slice_in_dim(tokens, me * share, share, 0).astype(F32)
    g_own = lax.dynamic_slice_in_dim(cotangent, me * share, share, 0).astype(F32)
    layer_out, grad_one, d_ctx, grad_down, grad_up, grad_out, up_bias, small = middle_part(
        parts, x_own, g_own, ctx_all, out_full, up_full, down_full,
        b_out.astype(F32), ln1_gain.astype(F32), ln1_bias.astype(F32), b_up_full,
        b_down.astype(F32), ln2_gain.astype(F32), ln2_bias.astype(F32),
    )
    d_ctx_own = lax.all_to_all(d_ctx, "tensor", 0, 0).reshape(rows, width)
    dq, dk, dv = backward_plain(q_t, k_n, v_t, lse, d_ctx_own, segment)
    d_qkv = jnp.stack([dq, dk, dv])
    grad_qkv_t = jnp.einsum("td,cte->dce", tokens, d_qkv, preferred_element_type=F32)
    qkv_bias = jnp.sum(d_qkv.astype(F32), axis=1)
    partial_input = jnp.einsum("cte,cde->td", d_qkv, w_qkv, preferred_element_type=F32)
    input_share = lax.psum_scatter(
        partial_input.astype(BF16), "tensor", scatter_dimension=0, tiled=True
    ).astype(F32)
    input_grad = (input_share + grad_one).astype(BF16)
    bias_grads = lax.psum(jnp.stack([qkv_bias[0], qkv_bias[2]]), "dp")
    up_bias_grad = lax.psum(lax.psum_scatter(up_bias, "tensor", scatter_dimension=0, tiled=True), "dp")[0]
    small_share = lax.psum_scatter(lax.psum(small, "tensor"), "dp", scatter_dimension=1, tiled=True)
    qkv_share = lax.psum_scatter(grad_qkv_t, "dp", scatter_dimension=0, tiled=True)

    def shared(blocks):
        stacked = jnp.stack(blocks).astype(BF16)
        over = lax.psum_scatter(stacked, "dp", scatter_dimension=1, tiled=True)
        return lax.psum_scatter(over, "tensor", scatter_dimension=0, tiled=True)[0].astype(F32)

    return (
        layer_out,
        input_grad,
        jnp.transpose(qkv_share, (1, 0, 2)),
        bias_grads,
        shared(grad_out).T,
        small_share[0],
        small_share[1],
        small_share[2],
        shared(grad_up),
        up_bias_grad,
        shared(grad_down).T,
        small_share[3],
        small_share[4],
        small_share[5],
    )


def backward_plain(q_t, k_n, v_t, lse, d_ctx, segment):
    width, rows = q_t.shape
    heads = width // HD
    queries = q_t.T.reshape(rows, heads, HD)
    keys = k_n.reshape(rows, heads, HD)
    values = v_t.T.reshape(rows, heads, HD)
    upstream = d_ctx.reshape(rows, heads, HD)
    scale = HD ** (-0.5)
    scores = jnp.einsum("qhd,khd->hqk", queries, keys, preferred_element_type=F32) * scale
    scores = jnp.where((segment[:, None] == segment[None, :])[None], scores, -1e30)
    soft = jnp.exp(scores - lse[..., None])
    dv = jnp.einsum("hqk,qhd->khd", soft.astype(BF16), upstream, preferred_element_type=F32)
    dp = jnp.einsum("qhd,khd->hqk", upstream, values, preferred_element_type=F32)
    ds = (soft * (dp - jnp.sum(dp * soft, axis=-1, keepdims=True))).astype(BF16)
    dq = jnp.einsum("hqk,khd->qhd", ds, keys, preferred_element_type=F32) * scale
    dk = jnp.einsum("hqk,qhd->khd", ds, queries, preferred_element_type=F32) * scale
    return tuple(d.reshape(rows, width).astype(BF16) for d in (dq, dk, dv))


def solution(mesh):
    return jax.shard_map(
        per_device,
        mesh=mesh,
        in_specs=(
            P("dp", None),
            P("dp", None),
            P(None, None, "tensor"),
            P(None, "tensor"),
            P("tensor", None),
            P(),
            P(),
            P(),
            P(None, "tensor"),
            P("tensor"),
            P("tensor", None),
            P(),
            P(),
            P(),
            P("dp", None),
        ),
        out_specs=(
            P(("dp", "tensor"), None),
            P(("dp", "tensor"), None),
            P(None, "dp", "tensor"),
            P(None, "tensor"),
            P("tensor", "dp"),
            P("dp"),
            P("dp"),
            P("dp"),
            P("dp", "tensor"),
            P("tensor"),
            P("tensor", "dp"),
            P("dp"),
            P("dp"),
            P("dp"),
        ),
        check_vma=False,
    )
```

time: 901 us -> 557 us (0.62)
  waiting for transfers between devices: 499 us -> 123 us
  Pallas kernels: 0 us -> 65.4 us
  other arithmetic: 122 us -> 72.9 us
  local copies, waits for them, and re-layouts: 70.2 us -> 33.8 us
  blocking collectives: 14.7 us -> 47 us
  matrix products: 156 us -> 183 us
  loops' own time: 13.6 us -> 0 us
    psum x3 -> x0, waiting for transfers between devices: 355 us -> none  [the longest x1 119 us: per_device(): lax.psum(jnp.dot(context, w_out, preferred_element_type=jnp.float32).asty...]
    pallas_call x0 -> x1, Pallas kernels: none -> 65.4 us  [forward_part(): pl.pallas_call(functools.partial(forward_kernel, parts), out_shape=[jax.S...]
    reduce_scatter x4 -> x6, waiting for transfers between devices: 144 us -> 104 us  [the longest x1 60.8 us: per_device(): lax.psum_scatter(partial_input.astype(BF16), 'tensor', scatter_dimension=...]
    dot_general x40, matrix products: 156 us -> 183 us  [the longest x9 47.3 us: mm(): lax.dot_general(a, b, (((1,), (0,)), ((), ())), preferred_element_type=F32)]
    reduce_sum x8 -> x3, other arithmetic: 28 us -> 5.08 us  [the longest x1 2.29 us: middle_part(): jnp.sum(grad_two, axis=0)]
    unnamed x0 -> x1, blocking collectives: none -> 19.4 us
    unnamed x11 -> x12, waiting for transfers between devices: 0.15 us -> 19.2 us
    dynamic_update_slice x8 -> x0, other arithmetic: 16.4 us -> none  [the longest x4 13.9 us: backward_block(): lax.dynamic_update_slice_in_dim(gathered_grads, current + update, offset, 1)]
  transfers between devices with their start and end apart: 9 -> 10, of which waited for: 6 -> 4; matrix products, arithmetic and copies ran while one was open for 22% -> 36% of each run, Pallas kernels for 0% -> 0%
where the time goes in v1:
time: 557 us; the launch traced here: 548 us
  matrix products  183 us (33%)
  waiting for transfers between devices  123 us (22%)
  other arithmetic  72.9 us (13%)
  Pallas kernels  65.4 us (12%)
  blocking collectives  47 us (8%)
  local copies, waits for them, and re-layouts  33.8 us (6%)
  between operations  15.1 us (3%)
  starting transfers between devices  7.88 us (1%)
    pallas_call x1, Pallas kernels, forward_part(): pl.pallas_call(functools.partial(forward_kernel, parts), out_shape=[jax.S...  65.4 us
    reduce_scatter x1, waiting for transfers between devices, per_device(): lax.psum_scatter(partial_input.astype(BF16), 'tensor', scatter_dimension=...  60.8 us
    dot_general x9, matrix products, mm(): lax.dot_general(a, b, (((1,), (0,)), ((), ())), preferred_element_type=F32)  47.3 us
    reduce_scatter x3, waiting for transfers between devices, shared(): lax.psum_scatter(over, 'tensor', scatter_dimension=0, tiled=True)[0]  43.4 us
    convert_element_type x1, other arithmetic, backward_plain(): ds = (soft * (dp - jnp.sum(dp * soft, axis=-1, keepdims=True))).astype(BF16)  42.9 us
    dot_general x1, matrix products, backward_plain(): jnp.einsum('qhd,khd->hqk', upstream, values, preferred_element_type=F32)  36.1 us
    unnamed x96, local copies, waits for them, and re-layouts  23 us
    dot_general x1, matrix products, backward_plain(): jnp.einsum('hqk,qhd->khd', soft.astype(BF16), upstream, preferred_element...  22 us
  transfers between devices with their start and end apart: 10, of which 4 were waited for; matrix products, arithmetic and copies ran while one was open for 36% of the time, Pallas kernels for 0%

profile of v1, /device:TPU:0, one launch (start us, length us, event | category | flops | bytes accessed | tf_op | source)
XLA Modules:
  0.0 548.2 jit_solution(14498723550407202273)
XLA Ops:
  13.6 14.8 %all-gather.1 = bf16[4,1,768]{2,1,0:T(2,128)(2,1)S(1)} all-gather(bf16[1,1,768]{2,1,0:T(2,128)(2,1)S(1)} %reshape.241), channel_id=2, replica_groups=mesh['dp'=8,'tensor'=4] {'tensor'}, dimensions={0}, use_global_device_ids=true | all-gather | bytes 7680 | tf_op jit(solution)/shard_map/all_gather | solution.py:340
  29.4 2.3 copy.54.wqkv
  31.7 2.3 broadcast_in_dim.19.seg_col
  33.9 65.4 %forward_part.1 = (bf16[192,2048]{1,0:T(8,128)(2,1)}, bf16[2048,192]{1,0:T(8,128)(2,1)}, bf16[192,2048]{1,0:T(8,128)(2,1)}, f32[3,2048]{1,0:T(4,128)}, bf16[4,51...) custom-call(bf16[2048,768]{1,0:T(8,128)(2,1)} %tok.1, ...), custom_call_target="tpu_custom_call" | custom-call | tf_op jit(solution)/shard_map/forward_part/pallas_call | solution.py:210
  99.4 1.6 copy.56
  101.0 2.2 fusion.80
  103.5 2.8 fusion.76
  106.7 10.2 %multiply_convert_fusion.1 = (bf16[512,768]{1,0:T(8,128)(2,1)S(1)}, f32[512,768]{1,0:T(8,128)S(1)}, f32[512,768]{1,0:T(8,128)S(1)}) fusion(f32[768]{0:T(1024)S(1)} %get-tuple-element.94, bf16[512,768]{1,0:T(8,128)(2,1)S(1)} %fusion.50, bf16[768,768]{1,0:T(8,128)(2,1)S(1)} %bitcast.212), kind=kOutput, calls=%fused_computation.53 | convolution fusion | flops 629932032 | bytes 5901312 | tf_op jit(solution)/shard_map/dot_general | solution.py:21
  117.0 10.4 %multiply_convert_fusion.2 = (bf16[512,768]{1,0:T(8,128)(2,1)S(1)}, f32[512,768]{1,0:T(8,128)S(1)}, f32[512,768]{1,0:T(8,128)S(1)}) fusion(f32[768]{0:T(1024)S(1)} %get-tuple-element.95, bf16[512,768]{1,0:T(8,128)(2,1)S(1)} %fusion.50, bf16[768,768]{1,0:T(8,128)(2,1)S(1)} %bitcast.221), kind=kOutput, calls=%fused_computation.66 | convolution fusion | flops 629932032 | bytes 5901312 | tf_op jit(solution)/shard_map/dot_general | solution.py:21
  128.3 10.2 %multiply_convert_fusion.3 = (bf16[512,768]{1,0:T(8,128)(2,1)S(1)}, f32[512,768]{1,0:T(8,128)S(1)}, f32[512,768]{1,0:T(8,128)S(1)}) fusion(f32[768]{0:T(1024)S(1)} %get-tuple-element.96, bf16[512,768]{1,0:T(8,128)(2,1)S(1)} %fusion.50, bf16[768,768]{1,0:T(8,128)(2,1)S(1)} %bitcast.229), kind=kOutput, calls=%fused_computation.79 | convolution fusion | flops 629932032 | bytes 5901312 | tf_op jit(solution)/shard_map/dot_general | solution.py:21
  139.4 10.6 %multiply_convert_fusion.4 = (bf16[512,768]{1,0:T(8,128)(2,1)S(1)}, f32[512,768]{1,0:T(8,128)S(1)}, f32[512,768]{1,0:T(8,128)S(1)}) fusion(f32[768]{0:T(1024)S(1)} %get-tuple-element.97, bf16[512,768]{1,0:T(8,128)(2,1)S(1)} %fusion.50, bf16[768,768]{1,0:T(8,128)(2,1)S(1)} %bitcast.225), kind=kOutput, calls=%fused_computation.92 | convolution fusion | flops 629932032 | bytes 5901312 | tf_op jit(solution)/shard_map/dot_general | solution.py:21
  150.9 1.2 fusion.81
  153.6 2.3 fusion.69
  156.0 1.8 convert_reduce_fusion.4
  158.7 1.8 convert_reduce_fusion.5
  161.4 1.8 convert_reduce_fusion.3
  164.1 1.8 convert_reduce_fusion.2
  165.8 1.6 multiply_reduce_fusion.1
  168.7 1.7 copy-done.5
  173.3 2.2 reshape.252
  175.6 2.0 fusion.43
  180.7 2.5 pad_maximum_fusion
  183.2 1.3 copy-done.9
  187.2 7.3 %all-to-all-start = ((bf16[4,512,192]{1,2,0:T(8,128)(2,1)}), bf16[4,512,192]{1,2,0:T(8,128)(2,1)S(1)}, u32[]{:S(2)}, u32[]{:S(2)}) async-start(bf16[4,512,192]{1,2,0:T(8,128)(2,1)} %pad_maximum_fusion.4), calls=%async_computation | async-start | bytes 1572864 | tf_op jit(solution)/shard_map/all_to_all | solution.py:348
  199.9 2.5 pad_maximum_fusion.1
  202.5 1.2 copy-done.10
  204.4 20.1 %fusion.85 = f32[3,2048,2048]{1,2,0:T(8,128)} fusion(bf16[2048,3,64]{0,2,1:T(8,128)(2,1)S(1)} %bitcast.209, bf16[2048,3,64]{0,2,1:T(8,128)(2,1)S(1)} %bitcast.201), kind=kOutput, calls=%fused_computation.202 | convolution fusion | flops 1610612736 | bytes 51904512 | tf_op jit(solution)/shard_map/qhd,khd->hqk/dot_general | solution.py:394
  224.5 4.2 broadcast_compare_fusion
  229.9 36.1 %multiply_reduce_fusion = (f32[3,2048]{1,0:T(4,128)S(1)}, f32[3,2048,2048]{1,2,0:T(8,128)}) fusion(f32[3,2048,2048]{1,2,0:T(8,128)} %fusion.85, f32[3,2048]{1,0:T(4,128)S(1)} %copy-done.21, pred[2048,2048]{0,1:T(8,128)(4,1)} %broadcast_compare_fusion, bf16[2048,3,64]{0,2,1:T(8,128)(2,1)S(1)} %reshape_reshape.7, bf16[2048,3,64]{0,2,1:T(8,128)(2,1)} %bitcast.239), kind=kOutput, calls=%fused_computation.1 | convolution fusion | flops 1673521152 | bytes 106479616 | tf_op jit(solution)/shard_map/qhd,khd->hqk/dot_general | solution.py:398
  265.9 42.9 %multiply_convert_fusion = bf16[3,2048,2048]{1,2,0:T(8,128)(2,1)} fusion(f32[3,2048,2048]{1,2,0:T(8,128)} %get-tuple-element.153, f32[3,2048,2048]{1,2,0:T(8,128)} %fusion.85, f32[3,2048]{1,0:T(4,128)S(1)} %get-tuple-element.152, f32[3,2048]{1,0:T(4,128)S(1)} %copy-done.21, pred[2048,2048]{0,1:T(8,128)(4,1)} %broadcast_compare_fusion), kind=kLoop, calls=%fused_computation | loop fusion | flops 75497472 | bytes 130072576 | tf_op jit(solution)/shard_map/convert_element_type | solution.py:399
  308.9 12.8 %fusion.7 = bf16[3,64,2048]{2,1,0:T(8,128)(2,1)S(1)} fusion(bf16[2048,3,64]{0,2,1:T(8,128)(2,1)S(1)} %bitcast.210, bf16[3,2048,2048]{1,2,0:T(8,128)(2,1)} %multiply_convert_fusion), kind=kOutput, calls=%fused_computation.16 | convolution fusion | flops 1611399168 | bytes 26738688 | tf_op jit(solution)/shard_map/hqk,qhd->khd/dot_general | solution.py:401
  321.7 11.6 %fusion.6 = bf16[3,64,2048]{2,1,0:T(8,128)(2,1)S(1)} fusion(bf16[2048,3,64]{0,2,1:T(8,128)(2,1)S(1)} %bitcast.202, bf16[3,2048,2048]{1,2,0:T(8,128)(2,1)} %multiply_convert_fusion), kind=kOutput, calls=%fused_computation.15 | convolution fusion | flops 1611399168 | bytes 26738688 | tf_op jit(solution)/shard_map/hqk,khd->qhd/dot_general | solution.py:400
  333.3 22.0 %fusion.8 = bf16[3,64,2048]{2,1,0:T(8,128)(2,1)} fusion(bf16[2048,3,64]{0,2,1:T(8,128)(2,1)S(1)} %copy-done.7, f32[3,2048,2048]{1,2,0:T(8,128)} %fusion.85, f32[3,2048]{1,0:T(4,128)S(1)} %copy-done.21, pred[2048,2048]{0,1:T(8,128)(4,1)S(1)} %copy-done), kind=kOutput, calls=%fused_computation.17 | convolution fusion | flops 1661337600 | bytes 56123392 | tf_op jit(solution)/shard_map/hqk,qhd->khd/dot_general | solution.py:397
  355.3 1.2 reshape.253
  357.4 5.3 fusion.4
  362.8 2.8 copy.72
  366.7 5.5 bitcast_convert_fusion
  374.7 19.4 %all-reduce.3 = (f32[4,768]{1,0:T(4,128)S(1)}, f32[6,96]{1,0:T(8,128)S(1)}) all-reduce(f32[4,768]{1,0:T(4,128)S(1)} %pad_maximum_fusion.5, f32[6,96]{1,0:T(8,128)S(1)} %copy.71), channel_id=10, replica_groups=mesh['dp'=8,'tensor'=4] {'tensor'}, use_global_device_ids=true, to_apply=%region_31.32.clone | all-reduce | flops 3648 | bytes 29184
  395.3 1.7 convert_reduce_fusion
  397.0 12.7 %all-reduce.2 = (f32[2,192]{1,0:T(2,128)}, f32[768]{0:T(1024)}) all-reduce(f32[2,192]{1,0:T(2,128)S(1)} %pad_maximum_fusion.6, f32[768]{0:T(1024)S(1)} %dynamic-slice_reduce_fusion), channel_id=1, replica_groups=mesh['dp'=8,'tensor'=4] {'dp'}, use_global_device_ids=true, to_apply=%region_14.15 | all-reduce | flops 1152 | bytes 9216 | tf_op jit(solution)/shard_map/psum | solution.py:358
  409.7 1.4 convert_bitcast_fusion.1
  411.2 18.4 %reduce-scatter.28.cloned.1.call-done = f32[96,576]{1,0:T(8,128)} async-done(((f32[768,576]{1,0:T(8,128)}), f32[96,576]{1,0:T(8,128)}) %reduce-scatter.28.cloned.1.call-update) | async-done | bytes 221200
  431.6 60.8 %reduce-scatter.16.cloned.1.call-done = bf16[512,768]{1,0:T(8,128)(2,1)} async-done(((bf16[2048,768]{1,0:T(8,128)(2,1)}), bf16[512,768]{1,0:T(8,128)(2,1)}) %reduce-scatter.16.cloned.1.call-update) | async-done | bytes 786448 | tf_op jit(solution)/shard_map/reduce_scatter | solution.py:354
  492.3 2.2 add_convert_fusion
  494.5 22.2 %reduce-scatter.22.cloned.1.call-done = bf16[1,96,768]{2,1,0:T(8,128)(2,1)} async-done(((bf16[4,96,768]{2,1,0:T(8,128)(2,1)}), bf16[1,96,768]{2,1,0:T(8,128)(2,1)}) %reduce-scatter.22.cloned.1.call-update) | async-done | bytes 147472 | tf_op jit(solution)/shard_map/reduce_scatter | solution.py:366
  516.7 1.6 bitcast_convert_fusion.1
  518.3 21.2 %reduce-scatter.26.cloned.1.call-done = bf16[1,96,768]{2,1,0:T(8,128)(2,1)} async-done(((bf16[4,96,768]{2,1,0:T(8,128)(2,1)}), bf16[1,96,768]{2,1,0:T(8,128)(2,1)}) %reduce-scatter.26.cloned.1.call-update) | async-done | bytes 147472 | tf_op jit(solution)/shard_map/reduce_scatter | solution.py:366
  539.5 1.6 convert_bitcast_fusion
  (184 shorter events, 39.5 us)
Async XLA Ops:
  7.2 348.1 %reduce-scatter.30.cloned.1.call-start = ((), (), s32[]{:S(2)}) async-start(), calls=%async_computation.17 | async-start | bytes 1327104
  13.6 20.3 %copy-start.22 = (s32[2048]{0:T(1024)}, s32[2048]{0:T(1024)S(1)}, u32[]{:S(2)}) copy-start(s32[2048]{0:T(1024)S(1)} %convert_reduce_fusion.6) | copy-start | bytes 24580
  99.4 1.6 copy-start.8
  101.0 2.6 copy-start.4
  106.7 32.7 %copy-start.14 = (bf16[512,768]{1,0:T(8,128)(2,1)}, bf16[512,768]{1,0:T(8,128)(2,1)S(1)}, u32[]{:S(2)}) copy-start(bf16[512,768]{1,0:T(8,128)(2,1)S(1)} %fusion.50) | copy-start | bytes 2359300
  116.9 34.0 %copy-start.17 = (bf16[512,768]{1,0:T(8,128)(2,1)}, bf16[512,768]{1,0:T(8,128)(2,1)S(1)}, u32[]{:S(2)}) copy-start(bf16[512,768]{1,0:T(8,128)(2,1)S(1)} %get-tuple-element.114) | copy-start | bytes 2359300
  127.4 0.9 copy-start.31
  150.0 0.9 copy-start.35
  150.9 1.9 copy-start.16
  156.0 8.1 %copy-start.12 = (bf16[512,768]{1,0:T(8,128)(2,1)}, bf16[512,768]{1,0:T(8,128)(2,1)S(1)}, u32[]{:S(2)}) copy-start(bf16[512,768]{1,0:T(8,128)(2,1)S(1)} %convert_element_type.190) | copy-start | bytes 2359300
  160.4 0.9 copy-start.38
  163.1 0.9 copy-start.40
  165.8 1.6 copy-start.19
  168.6 2.2 copy-start.1
  168.6 1.8 copy-start.5
  173.3 2.3 copy-start.15
  175.5 2.1 copy-start.39
  175.5 196.8 %reduce-scatter.20.cloned.1.call-start = ((), (), s32[]{:S(2)}) async-start(), calls=%async_computation.12 | async-start | bytes 5308416 | tf_op jit(solution)/shard_map/reduce_scatter | solution.py:365
  177.6 1.1 copy-start.20
  178.7 1.1 copy-start.41
  183.2 1.3 copy-start.9
  186.2 8.3 %copy-start.25 = (f32[768]{0:T(1024)S(1)}, f32[768]{0:T(1024)}, u32[]{:S(2)}) copy-start(f32[768]{0:T(1024)} %get-tuple-element.102) | copy-start | bytes 9220
  186.3 8.3 %copy-start.24 = (f32[768]{0:T(1024)S(1)}, f32[768]{0:T(1024)}, u32[]{:S(2)}) copy-start(f32[768]{0:T(1024)} %get-tuple-element.104) | copy-start | bytes 9220
  187.2 8.5 %copy-start.13 = (bf16[512,768]{1,0:T(8,128)(2,1)S(1)}, bf16[512,768]{1,0:T(8,128)(2,1)}, u32[]{:S(2)}) copy-start(bf16[512,768]{1,0:T(8,128)(2,1)} %copy-done.12) | copy-start | bytes 2359300
  187.2 8.5 %copy-start.18 = (bf16[512,768]{1,0:T(8,128)(2,1)S(1)}, bf16[512,768]{1,0:T(8,128)(2,1)}, u32[]{:S(2)}) copy-start(bf16[512,768]{1,0:T(8,128)(2,1)} %copy-done.17) | copy-start | bytes 2359300
  187.2 41.4 %all-to-all-start = ((bf16[4,512,192]{1,2,0:T(8,128)(2,1)}), bf16[4,512,192]{1,2,0:T(8,128)(2,1)S(1)}, u32[]{:S(2)}, u32[]{:S(2)}) async-start(bf16[4,512,192]{1,2,0:T(8,128)(2,1)} %pad_maximum_fusion.4), calls=%async_computation | async-start | bytes 1572864 | tf_op jit(solution)/shard_map/all_to_all | solution.py:348
  194.5 179.3 %reduce-scatter.32.cloned.1.call-start = ((), (), s32[]{:S(2)}) async-start(), calls=%async_computation.18 | async-start | bytes 442368
  195.6 1.1 copy-start.32
  195.6 199.7 %reduce-scatter.24.cloned.1.call-start = ((), (), s32[]{:S(2)}) async-start(), calls=%async_computation.14 | async-start | bytes 5308416 | tf_op jit(solution)/shard_map/reduce_scatter | solution.py:365
  196.8 1.2 copy-start.34
  198.0 1.1 copy-start.36
  202.4 1.2 copy-start.10
  202.4 1.9 copy-start.3
  202.5 207.3 %reduce-scatter.18.cloned.1.call-start = ((), (), s32[]{:S(2)}) async-start(), calls=%async_computation.11 | async-start | bytes 245760 | tf_op jit(solution)/shard_map/reduce_scatter | solution.py:366
  204.4 20.1 %copy-start.23 = (s32[2048]{0:T(1024)S(1)}, s32[2048]{0:T(1024)}, u32[]{:S(2)}) copy-start(s32[2048]{0:T(1024)} %copy-done.22) | copy-start | bytes 24580
  228.6 1.2 copy-start.21
  229.8 36.1 %copy-start.6 = (bf16[2048,3,64]{0,2,1:T(8,128)(2,1)}, bf16[2048,3,64]{0,2,1:T(8,128)(2,1)S(1)}, u32[]{:S(2)}) copy-start(bf16[2048,3,64]{0,2,1:T(8,128)(2,1)S(1)} %reshape_reshape.7) | copy-start | bytes 2359300
  321.6 11.7 %copy-start = (pred[2048,2048]{0,1:T(8,128)(4,1)S(1)}, pred[2048,2048]{0,1:T(8,128)(4,1)}, u32[]{:S(2)}) copy-start(pred[2048,2048]{0,1:T(8,128)(4,1)} %broadcast_compare_fusion) | copy-start | bytes 12582916
  321.6 11.7 %copy-start.7 = (bf16[2048,3,64]{0,2,1:T(8,128)(2,1)S(1)}, bf16[2048,3,64]{0,2,1:T(8,128)(2,1)}, u32[]{:S(2)}) copy-start(bf16[2048,3,64]{0,2,1:T(8,128)(2,1)} %copy-done.6) | copy-start | bytes 2359300
  357.4 72.2 %reduce-scatter.28.cloned.1.call-start = ((), (), s32[]{:S(2)}) async-start(), calls=%async_computation.16 | async-start | bytes 2211840
  365.6 1.2 copy-start.11
  365.6 126.8 %reduce-scatter.16.cloned.1.call-start = ((), (), s32[]{:S(2)}) async-start(), calls=%async_computation.10 | async-start | bytes 3932160 | tf_op jit(solution)/shard_map/reduce_scatter | solution.py:354
  372.2 0.9 copy-start.26
  372.2 0.9 copy-start.29
  372.2 0.9 copy-start.30
  372.2 144.4 %reduce-scatter.22.cloned.1.call-start = ((), (), s32[]{:S(2)}) async-start(), calls=%async_computation.13 | async-start | bytes 737280 | tf_op jit(solution)/shard_map/reduce_scatter | solution.py:366
  373.0 166.5 %reduce-scatter.26.cloned.1.call-start = ((), (), s32[]{:S(2)}) async-start(), calls=%async_computation.15 | async-start | bytes 737280 | tf_op jit(solution)/shard_map/reduce_scatter | solution.py:366
  395.3 97.0 %copy-start.2 = (f32[512,768]{1,0:T(8,128)S(1)}, f32[512,768]{1,0:T(8,128)}, u32[]{:S(2)}) copy-start(f32[512,768]{1,0:T(8,128)} %copy-done.1) | copy-start | bytes 4718596
  (4 other events, 3.5 us)
Sparse Core Ops, SparseCore 0:
  175.6 38.4 reduce-scatter.29
  217.6 53.7 reduce-scatter.19
  274.5 33.8 reduce-scatter.31
  311.7 53.7 reduce-scatter.23
  368.2 19.6 reduce-scatter.17
  391.2 38.3 reduce-scatter.27
  431.9 60.4 reduce-scatter.15
  494.6 22.0 reduce-scatter.21
  519.0 20.5 reduce-scatter.25

commit v2 on v1

--- a/solution.py
+++ b/solution.py
@@ -56,9 +56,9 @@
 
 
 def forward_kernel(
-    parts, tok, wqkv, bias, seg_row, seg_col, up, down, out,
-    q_t, k_n, v_t, lse, ctx_all, up_all, down_all, out_all,
-    k_pad, v_pad, ctx, z_send, z_recv, x_send, x_recv, c_send, c_recv, a_send, a_recv, l_sem,
+    parts, tok, wqkv, bias, seg_row, seg_col, b_up, up, down, out,
+    q_t, k_n, v_t, lse, ctx_all, b_all, up_all, down_all, out_all,
+    k_pad, v_pad, ctx, z_send, z_recv, x_send, x_recv, c_send, c_recv, a_send, a_recv, b_send, b_recv, l_sem,
 ):
     rows = tok.shape[0]
     width = wqkv.shape[2]
@@ -82,19 +82,26 @@
             shards[w].at[rank], fulls[w].at[me, rank], z_send.at[w, j - 1], z_recv.at[w, j - 1], (dp, at(j))
         )
 
-    def x_copy(w, j, k, slot):
-        source = at(parts - j)
-        piece = fulls[w].at[source, slot]
-        return remote(piece, piece, x_send.at[w, j - 1, k], x_recv.at[w, j - 1, k], (base + others[1 + k], me))
+    def x_copy(w, j, k, slot, to):
+        piece = fulls[w].at[at(parts - j), slot]
+        return remote(piece, piece, x_send.at[w, j - 1, k], x_recv.at[w, j - 1, k], (base + to, me))
+
+    through = (1, 1, 2)
 
     def c_copy(w, j, k, slot):
         source = at(parts - j)
         piece = fulls[w].at[source, slot]
         return remote(piece, piece, c_send.at[w, j - 1, k], c_recv.at[w, j - 1, k], (base + others[0], me))
 
+    def b_copy(j):
+        return remote(b_up, b_all.at[me], b_send.at[j - 1], b_recv.at[j - 1], (dp, at(j)))
+
+    for j in range(1, parts):
+        b_copy(j).start()
     for w in range(3):
         for j in range(1, parts):
             z_copy(w, j).start()
+    b_all[me] = b_up[...]
     own = [pltpu.make_async_copy(shards[w], fulls[w].at[me], l_sem.at[w]) for w in range(3)]
     for copy in own:
         copy.start()
@@ -102,15 +109,25 @@
     def spread(w):
         for j in range(1, parts):
             z_copy(w, j).wait_recv()
-            for k in range(3):
-                x_copy(w, j, k, rank).start()
+            for k in (1, 2):
+                x_copy(w, j, k, rank, others[k]).start()
+
+    def relay(w):
+        k = through[w]
+        for j in range(1, parts):
+            x_copy(w, j, k, others[k], others[k]).wait_recv()
+            x_copy(w, j, 0, others[k], others[3 - k]).start()
+            c_copy(w, j, 0, rank).start()
+            c_copy(w, j, k, others[k]).start()
 
     def pass_on(w):
-        for j in range(1, parts):
-            c_copy(w, j, 0, rank).start()
-            for k in range(3):
-                x_copy(w, j, k, others[1 + k]).wait_recv()
-                c_copy(w, j, 1 + k, others[1 + k]).start()
+        k = 3 - through[w]
+        for j in range(1, parts):
+            x_copy(w, j, k, others[k], others[k]).wait_recv()
+            c_copy(w, j, k, others[k]).start()
+        for j in range(1, parts):
+            x_copy(w, j, 0, others[3], others[k]).wait_recv()
+            c_copy(w, j, 3, others[3]).start()
 
     k_pad[:, :MOST] = jnp.zeros((heads, MOST, HD), BF16)
     k_pad[:, MOST + rows :] = jnp.zeros((heads, MOST, HD), BF16)
@@ -170,31 +187,34 @@
             def _(j=j):
                 a_copy(j).start()
 
-        @pl.when(step == 3)
-        def _():
-            spread(1)
+        for when, what, w in ((0, relay, 0), (1, spread, 1), (4, spread, 2), (5, relay, 1), (6, pass_on, 0)):
+
+            @pl.when(step == when)
+            def _(what=what, w=w):
+                what(w)
 
     keep = pltpu.make_async_copy(ctx.at[me], ctx_all.at[me], l_sem.at[3])
     keep.start()
-    spread(2)
-    for w in range(3):
-        pass_on(w)
+    relay(2)
+    pass_on(1)
+    pass_on(2)
     for j in range(1, parts):
         a_copy(j).wait()
+        b_copy(j).wait()
     for w in range(3):
         for j in range(1, parts):
             z_copy(w, j).wait_send()
-            c_copy(w, j, 0, rank).wait_send()
-            c_copy(w, j, 0, others[0]).wait_recv()
-            for k in range(3):
-                x_copy(w, j, k, rank).wait_send()
-                c_copy(w, j, 1 + k, others[1 + k]).wait()
+            for k in (1, 2):
+                x_copy(w, j, k, rank, others[k]).wait_send()
+            x_copy(w, j, 0, others[3], others[3 - through[w]]).wait_send()
+            for k in range(4):
+                c_copy(w, j, k, others[0]).wait()
     for copy in own:
         copy.wait()
     keep.wait()
 
 
-def forward_part(parts, tokens, w_qkv, bias, seg_row, seg_col, w_up, w_down, w_out):
+def forward_part(parts, tokens, w_qkv, bias, seg_row, seg_col, b_up, w_up, w_down, w_out):
     rows, model = tokens.shape
     width = w_qkv.shape[2]
     heads = width // HD
@@ -215,10 +235,11 @@
             jax.ShapeDtypeStruct((width, rows), BF16),
             jax.ShapeDtypeStruct((heads, rows), F32),
             jax.ShapeDtypeStruct((parts, share, width), BF16),
+            jax.ShapeDtypeStruct((parts,) + b_up.shape, F32),
         ]
         + [jax.ShapeDtypeStruct((parts,) + s.shape, BF16) for s in shards],
-        in_specs=[vmem] * 8,
-        out_specs=[vmem] * 5 + [hbm] * 3,
+        in_specs=[vmem] * 9,
+        out_specs=[vmem] * 6 + [hbm] * 3,
         scratch_shapes=[
             pltpu.VMEM((heads, rows + 2 * MOST, HD), BF16),
             pltpu.VMEM((width, rows + 2 * MOST), BF16),
@@ -231,20 +252,424 @@
             dma((3, parts - 1, 4)),
             dma((parts - 1,)),
             dma((parts - 1,)),
+            dma((parts - 1,)),
+            dma((parts - 1,)),
             dma((4,)),
         ],
         compiler_params=pltpu.CompilerParams(
             collective_id=0, has_side_effects=True, vmem_limit_bytes=60 * 1024 * 1024
         ),
         name="forward_part",
-    )(tokens, w_qkv, bias, seg_row, seg_col, *shards)
-    q_t, k_n, v_t, lse, ctx_all, up_all, down_all, out_all = outs
+    )(tokens, w_qkv, bias, seg_row, seg_col, b_up, *shards)
+    q_t, k_n, v_t, lse, ctx_all, b_all, up_all, down_all, out_all = outs
     return (
-        q_t, k_n, v_t, lse, ctx_all,
+        q_t, k_n, v_t, lse, ctx_all, b_all[:, 0],
         up_all.reshape((parts,) + w_up.shape),
         down_all.reshape((parts,) + w_down.shape),
         out_all.reshape((parts,) + w_out.shape),
     )
+
+
+def backward_kernel(
+    parts, d_ctx, q_t, k_n, v_t, lse, seg_row, seg_col, tok, wqkv, g_own, sums, g_down, g_up, g_out,
+    d_in, s_down, s_up, s_out, s_qkv, s_sums,
+    dc, k_pad, v_pad, k_t, q_n, acc_k, acc_v, dq_t, dk, dv, part, chain,
+    p_down, p_up, p_out, r_down, r_up, r_out, x_down, x_up, x_out, z_down, z_up, z_out,
+    gq, r_gq, x_gq, sum_z, sum_dp, sum_in,
+    a_send, a_recv, l_sem, s1_send, s1_recv, s2_send, s2_recv, s3_send, s3_recv,
+    h_send, h_recv, m_send, m_recv, n_send, n_recv,
+):
+    rows, model = tok.shape
+    width = wqkv.shape[2]
+    heads = width // HD
+    share = rows // parts
+    dp = lax.axis_index("dp")
+    me = lax.axis_index("tensor")
+    rank = dp % GROUP
+    base = dp - rank
+    core = rank % 2
+    chip = rank // 2
+    others = peers_of(rank)
+    full = (g_down, g_up, g_out)
+    held = (p_down, p_up, p_out, gq)
+    first = (r_down, r_up, r_out, r_gq)
+    second = (x_down, x_up, x_out, x_gq)
+    third = (z_down, z_up, z_out)
+    shared = (s_down, s_up, s_out)
+    scale = HD ** (-0.5)
+
+    def at(j):
+        return (me + j) % parts
+
+    fellows = [(rank + k) % GROUP for k in range(1, GROUP)]
+    greet([(dp, at(j)) for j in range(1, parts)] + [(base + f, me) for f in fellows])
+
+    def a_copy(j):
+        return remote(d_ctx.at[at(j)], dc.at[me], a_send.at[j - 1], a_recv.at[j - 1], (dp, at(j)))
+
+    def s1_copy(w):
+        src = full[w].at[:, :, 1 - core] if w < 3 else gq.at[:, 1 - core]
+        return remote(src, first[w], s1_send.at[w], s1_recv.at[w], (base + others[0], me))
+
+    def s2_copy(w, k):
+        to = others[1 + k]
+        src = held[w].at[:, to // 2] if w < 3 else gq.at[to // 2, core]
+        return remote(src, second[w].at[k], s2_send.at[w, k], s2_recv.at[w, k], (base + to, me))
+
+    def s3_copy(w, j):
+        return remote(
+            held[w].at[at(j), chip], third[w].at[j - 1], s3_send.at[w, j - 1], s3_recv.at[w, j - 1], (dp, at(j))
+        )
+
+    def m_copy(j):
+        return remote(sums, sum_z.at[j - 1], m_send.at[j - 1], m_recv.at[j - 1], (dp, at(j)))
+
+    def n_copy(k):
+        return remote(sum_in, sum_dp.at[k], n_send.at[k], n_recv.at[k], (base + fellows[k], me))
+
+    for j in range(1, parts):
+        a_copy(j).start()
+    for j in range(1, parts):
+        m_copy(j).start()
+    loads = [pltpu.make_async_copy(full[w].at[:, :, core], held[w], l_sem.at[w]) for w in range(3)]
+    for w in range(3):
+        s1_copy(w).start()
+        loads[w].start()
+    mine = pltpu.make_async_copy(d_ctx.at[me], dc.at[me], l_sem.at[3])
+    mine.start()
+
+    for ref in (k_pad, v_pad):
+        ref[:MOST, :] = jnp.zeros((MOST, width), BF16)
+        ref[MOST + rows :, :] = jnp.zeros((MOST, width), BF16)
+    k_t[:, :MOST] = jnp.zeros((width, MOST), BF16)
+    k_t[:, MOST + rows :] = jnp.zeros((width, MOST), BF16)
+
+    @pl.loop(0, rows // TILE)
+    def _(t):
+        here = pl.ds(pl.multiple_of(t * TILE, TILE), TILE)
+        there = pl.ds(pl.multiple_of(t * TILE + MOST, TILE), TILE)
+        keys = k_n[here, :]
+        k_pad[there, :] = keys
+        k_t[:, there] = keys.astype(F32).T.astype(BF16)
+        v_pad[there, :] = v_t[:, here].astype(F32).T.astype(BF16)
+        q_n[here, :] = (q_t[:, here].astype(F32) * scale).T.astype(BF16)
+
+    @pl.loop(0, (rows + 2 * MOST) // TILE)
+    def _(t):
+        here = pl.ds(pl.multiple_of(t * TILE, TILE), TILE)
+        acc_k[here, :] = jnp.zeros((TILE, width), F32)
+        acc_v[here, :] = jnp.zeros((TILE, width), F32)
+
+    def s1_finish(w):
+        s1_copy(w).wait_recv()
+        loads[w].wait()
+
+        @pl.loop(0, parts)
+        def _(n):
+            for c in range(GROUP // 2):
+                held[w][n, c] = (held[w][n, c].astype(F32) + first[w][n, c].astype(F32)).astype(BF16)
+
+        for k in range(3):
+            s2_copy(w, k).start()
+
+    def s2_finish(w):
+        for k in range(3):
+            s2_copy(w, k).wait_recv()
+
+        @pl.loop(0, parts)
+        def _(n):
+            total = held[w][n, chip].astype(F32)
+            for k in range(3):
+                total = total + second[w][k, n].astype(F32)
+            held[w][n, chip] = total.astype(BF16)
+
+        for j in range(1, parts):
+            s3_copy(w, j).start()
+
+    def s3_finish(w):
+        for j in range(1, parts):
+            s3_copy(w, j).wait_recv()
+        total = held[w][me, chip].astype(F32)
+        for j in range(1, parts):
+            total = total + third[w][j - 1].astype(F32)
+        shared[w][...] = total
+
+    span = TILE + 2 * MOST
+    per_block = share // TILE
+    mine.wait()
+
+    @pl.loop(0, rows // TILE)
+    def _(step):
+        for j in range(1, parts):
+
+            @pl.when(step == j * per_block)
+            def _(j=j):
+                a_copy(parts - j).wait_recv()
+
+        block = (me + step // per_block) % parts
+        inner = (step % per_block) * TILE
+        begin = block * share + inner
+        here = pl.ds(pl.multiple_of(begin, TILE), TILE)
+        window = pl.ds(pl.multiple_of(begin, TILE), span)
+        allowed_q = seg_row[:, here]
+        allowed_k = seg_col[window, :]
+        allowed = jnp.concatenate(
+            [allowed_k == allowed_q[:, i * 128 : (i + 1) * 128] for i in range(TILE // 128)], axis=1
+        )
+        up_n = dc[block, pl.ds(pl.multiple_of(inner, TILE), TILE), :]
+        up_t = up_n.astype(F32).T.astype(BF16)
+        grads_k = []
+        grads_v = []
+        for h in range(heads):
+            hs = slice(h * HD, (h + 1) * HD)
+            queries = q_t[hs, here] * jnp.asarray(scale, BF16)
+            scores = jnp.where(allowed, mm(k_pad[window, :][:, hs], queries), -1e30)
+            soft = jnp.exp(scores - lse[h : h + 1, here])
+            grad = mm(v_pad[window, :][:, hs], up_t[hs, :])
+            shift = jnp.sum(grad * soft, axis=0, keepdims=True)
+            inner_grad = (soft * (grad - shift)).astype(BF16)
+            grads_v.append(mm(soft.astype(BF16), up_n[:, hs]))
+            grads_k.append(mm(inner_grad, q_n[here, :][:, hs]))
+            dq_t[hs, here] = (mm(k_t[hs, window], inner_grad) * scale).astype(BF16)
+        acc_k[window, :] += jnp.concatenate(grads_k, axis=1)
+        acc_v[window, :] += jnp.concatenate(grads_v, axis=1)
+
+        @pl.when(step == 1)
+        def _():
+            s1_finish(0)
+
+        @pl.when(step == 3)
+        def _():
+            s1_finish(1)
+
+        @pl.when(step == 4)
+        def _():
+            s1_finish(2)
+
+        @pl.when(step == 6)
+        def _():
+            s2_finish(0)
+
+    @pl.loop(0, rows // TILE)
+    def _(t):
+        here = pl.ds(pl.multiple_of(t * TILE, TILE), TILE)
+        there = pl.ds(pl.multiple_of(t * TILE + MOST, TILE), TILE)
+        dk[here, :] = acc_k[there, :].astype(BF16)
+        dv[here, :] = acc_v[there, :].astype(BF16)
+
+    def own_part(b):
+        @pl.loop(0, per_block)
+        def _(t):
+            here = pl.ds(pl.multiple_of(b * share + t * TILE, TILE), TILE)
+            total = mm_tt(dq_t[:, here], wqkv[0]) + mm_nt(dk[here, :], wqkv[1]) + mm_nt(dv[here, :], wqkv[2])
+            part[b, pl.ds(pl.multiple_of(t * TILE, TILE), TILE), :] = total.astype(BF16)
+
+    def right_copy(b):
+        return remote(part.at[b], chain.at[b], h_send.at[0, b], h_recv.at[0, b], (dp, me + 1))
+
+    def left_copy(b):
+        slot = jnp.where(b == me - 1, parts, b)
+        return remote(part.at[b], chain.at[slot], h_send.at[1, b], h_recv.at[1, b], (dp, me - 1))
+
+    def fold(b):
+        @pl.loop(0, per_block)
+        def _(t):
+            here = pl.ds(pl.multiple_of(t * TILE, TILE), TILE)
+            part[b, here, :] = (part[b, here, :].astype(F32) + chain[b, here, :].astype(F32)).astype(BF16)
+
+    def go_right(b):
+        @pl.when(me < b)
+        def _():
+            @pl.when(me > 0)
+            def _():
+                right_copy(b).wait_recv()
+                fold(b)
+
+            right_copy(b).start()
+
+    def go_left(b):
+        @pl.when(me > b)
+        def _():
+            @pl.when(me < parts - 1)
+            def _():
+                remote(part.at[b], chain.at[b], h_send.at[1, b], h_recv.at[1, b], (dp, me - 1)).wait_recv()
+                fold(b)
+
+            left_copy(b).start()
+
+    own_part(parts - 1)
+    own_part(0)
+    go_right(parts - 1)
+    go_left(0)
+    for b in range(parts - 2, 0, -1):
+        own_part(b)
+    s2_finish(1)
+
+    for c in range(3):
+        if c == 0:
+            grads = mm(dq_t[...], tok[...])
+        else:
+            grads = mm_tn((dk, dv)[c - 1][...], tok[...])
+        grads = grads.T.astype(BF16)
+        deep = model // GROUP
+        for i in range(GROUP):
+            gq[i // 2, i % 2, c] = grads[i * deep : (i + 1) * deep, :]
+    remote(gq.at[:, 1 - core], r_gq, s1_send.at[3], s1_recv.at[3], (base + others[0], me)).start()
+    for j in range(1, parts):
+        m_copy(j).wait_recv()
+    total = sums[...]
+    for j in range(1, parts):
+        total = total + sum_z[j - 1]
+    sum_in[...] = total
+    keep = sum_in.shape[0] - 8
+    flat_q = jnp.sum(dq_t[...].astype(F32), axis=1, keepdims=True).T
+    flat_v = jnp.sum(dv[...].astype(F32), axis=0, keepdims=True)
+    sum_in[keep : keep + 1, :width] = flat_q
+    sum_in[keep + 1 : keep + 2, :width] = flat_v
+    for k in range(GROUP - 1):
+        n_copy(k).start()
+
+    go_right(parts - 2)
+    go_left(1)
+    s1_copy(3).wait_recv()
+    for c in range(GROUP // 2):
+        for i in range(3):
+            gq[c, core, i] = (gq[c, core, i].astype(F32) + r_gq[c, i].astype(F32)).astype(BF16)
+    for k in range(3):
+        s2_copy(3, k).start()
+    s2_finish(2)
+    for b in range(parts - 3, 0, -1):
+        go_right(b)
+    for b in range(2, parts - 1):
+        go_left(b)
+
+    for k in range(3):
+        s2_copy(3, k).wait_recv()
+    for i in range(3):
+        block = gq[chip, core, i].astype(F32)
+        for k in range(3):
+            block = block + x_gq[k, i].astype(F32)
+        s_qkv[i] = block
+    for k in range(GROUP - 1):
+        n_copy(k).wait()
+    total = sum_in[...]
+    for k in range(GROUP - 1):
+        total = total + sum_dp[k]
+    s_sums[...] = total
+    for w in range(3):
+        s3_finish(w)
+
+    @pl.when(me > 0)
+    def _():
+        remote(part.at[me], chain.at[me], h_send.at[0, me], h_recv.at[0, me], (dp, me)).wait_recv()
+        fold(me)
+
+    @pl.when(me < parts - 1)
+    def _():
+        remote(part.at[me], chain.at[parts], h_send.at[1, me], h_recv.at[1, me], (dp, me)).wait_recv()
+
+        @pl.loop(0, per_block)
+        def _(t):
+            here = pl.ds(pl.multiple_of(t * TILE, TILE), TILE)
+            part[me, here, :] = (part[me, here, :].astype(F32) + chain[parts, here, :].astype(F32)).astype(BF16)
+
+    @pl.loop(0, per_block)
+    def _(t):
+        here = pl.ds(pl.multiple_of(t * TILE, TILE), TILE)
+        d_in[here, :] = (part[me, here, :].astype(F32) + g_own[here, :]).astype(BF16)
+
+    for j in range(1, parts):
+        a_copy(j).wait_send()
+        m_copy(j).wait_send()
+    for w in range(4):
+        s1_copy(w).wait_send()
+        for k in range(3):
+            s2_copy(w, k).wait_send()
+    for w in range(3):
+        for j in range(1, parts):
+            s3_copy(w, j).wait_send()
+    for b in range(1, parts):
+
+        @pl.when(me < b)
+        def _(b=b):
+            right_copy(b).wait_send()
+
+    for b in range(parts - 1):
+
+        @pl.when(me > b)
+        def _(b=b):
+            left_copy(b).wait_send()
+
+
+def backward_part(parts, d_ctx, q_t, k_n, v_t, lse, seg_row, seg_col, tokens, w_qkv, g_own, sums, grads):
+    rows, model = tokens.shape
+    width = w_qkv.shape[2]
+    heads = width // HD
+    share = rows // parts
+    deep = model // GROUP
+    wides = [g.shape[2] for g in grads]
+    blocks = [g.reshape(parts, GROUP // 2, 2, deep, g.shape[2]) for g in grads]
+    vmem = pl.BlockSpec(memory_space=pltpu.VMEM)
+    hbm = pl.BlockSpec(memory_space=pl.ANY)
+    dma = pltpu.SemaphoreType.DMA
+    padded = rows + 2 * MOST
+
+    def held(*lead):
+        return [pltpu.VMEM(lead + (deep, w), BF16) for w in wides]
+
+    return pl.pallas_call(
+        functools.partial(backward_kernel, parts),
+        out_shape=[jax.ShapeDtypeStruct((share, model), BF16)]
+        + [jax.ShapeDtypeStruct((deep, w), F32) for w in wides]
+        + [jax.ShapeDtypeStruct((3, deep, width), F32), jax.ShapeDtypeStruct(sums.shape, F32)],
+        in_specs=[vmem] * 11 + [hbm] * 3,
+        out_specs=[vmem] * 6,
+        scratch_shapes=[
+            pltpu.VMEM((parts, share, width), BF16),
+            pltpu.VMEM((padded, width), BF16),
+            pltpu.VMEM((padded, width), BF16),
+            pltpu.VMEM((width, padded), BF16),
+            pltpu.VMEM((rows, width), BF16),
+            pltpu.VMEM((padded, width), F32),
+            pltpu.VMEM((padded, width), F32),
+            pltpu.VMEM((width, rows), BF16),
+            pltpu.VMEM((rows, width), BF16),
+            pltpu.VMEM((rows, width), BF16),
+            pltpu.VMEM((parts, share, model), BF16),
+            pltpu.VMEM((parts + 1, share, model), BF16),
+        ]
+        + held(parts, GROUP // 2)
+        + held(parts, GROUP // 2)
+        + held(3, parts)
+        + held(parts - 1)
+        + [
+            pltpu.VMEM((GROUP // 2, 2, 3, deep, width), BF16),
+            pltpu.VMEM((GROUP // 2, 3, deep, width), BF16),
+            pltpu.VMEM((3, 3, deep, width), BF16),
+            pltpu.VMEM((parts - 1,) + sums.shape, F32),
+            pltpu.VMEM((GROUP - 1,) + sums.shape, F32),
+            pltpu.VMEM(sums.shape, F32),
+            dma((parts - 1,)),
+            dma((parts - 1,)),
+            dma((4,)),
+            dma((4,)),
+            dma((4,)),
+            dma((4, 3)),
+            dma((4, 3)),
+            dma((3, parts - 1)),
+            dma((3, parts - 1)),
+            dma((2, parts)),
+            dma((2, parts)),
+            dma((parts - 1,)),
+            dma((parts - 1,)),
+            dma((GROUP - 1,)),
+            dma((GROUP - 1,)),
+        ],
+        compiler_params=pltpu.CompilerParams(
+            collective_id=1, has_side_effects=True, vmem_limit_bytes=64 * 1024 * 1024 - 128 * 1024
+        ),
+        name="backward_part",
+    )(d_ctx, q_t, k_n, v_t, lse, seg_row, seg_col, tokens, w_qkv, g_own, sums, *blocks)
 
 
 def segment_ids(pair_lengths, count):
@@ -261,48 +686,168 @@
     return (normed * gain + shift_bias, normed, inv_spread)
 
 
-def norm_backward(upstream, normed, inv_spread, gain):
-    scaled = upstream * gain
-    adjusted = (
-        scaled
-        - jnp.mean(scaled, axis=-1, keepdims=True)
-        - normed * jnp.mean(scaled * normed, axis=-1, keepdims=True)
-    )
-    return (adjusted * inv_spread, jnp.sum(upstream * normed, axis=0), jnp.sum(upstream, axis=0))
-
-
-def gelu_exact(value):
-    return jax.nn.gelu(value, approximate=False)
-
-
-def middle_part(parts, x_own, g_own, ctx_all, w_out, w_up, w_down, b_out, g1, s1, b_up, b_down, g2, s2):
+def middle_kernel(
+    parts, x, g, ctx, vecs, b_up, out_hbm, up_hbm, down_hbm,
+    layer_out, grad_one, d_ctx, sums, g_down, g_up, g_out,
+    out, up, down, act, slope, low, low_t, hid, normed, inv, fed, d_fed, d_fed_t, d_pre,
+    v_down, v_up, v_out, l_sem, s_sem,
+):
+    own, model = x.shape
+    half = own // 2
+    loads = [
+        pltpu.make_async_copy(a.at[n], b.at[n], l_sem.at[i, n])
+        for i, (a, b) in enumerate(((out_hbm, out), (up_hbm, up), (down_hbm, down)))
+        for n in range(parts)
+    ]
+    for load in loads:
+        load.start()
+    b_out, g1, s1, b_down, g2, s2 = [vecs[i : i + 1, :] for i in range(6)]
+    sums[...] = jnp.zeros(sums.shape, F32)
+    for load in loads[:parts]:
+        load.wait()
+
+    def rows_of(r):
+        return pl.ds(pl.multiple_of(r * half, half), half)
+
+    def add_to(row, values):
+        sums[row : row + 1, :] += jnp.sum(values, axis=0, keepdims=True)
+
+    @pl.loop(0, 2)
+    def _(r):
+        here = rows_of(r)
+        mixed = x[here, :].astype(F32) + b_out
+        for n in range(parts):
+            mixed = mixed + mm(ctx[n, here, :], out[n])
+        value, n1, r1 = norm_forward(mixed, g1, s1)
+        hid[here, :] = value
+        normed[here, :] = n1
+        inv[here, :] = jnp.broadcast_to(r1, (half, 128))
+        low[here, :] = value.astype(BF16)
+        low_t[:, here] = value.T.astype(BF16)
+        fed[here, :] = value + b_down
+
+    for load in loads[parts:]:
+        load.wait()
+
+    @pl.loop(0, parts * 2)
+    def _(t):
+        n = t // 2
+        here = rows_of(t % 2)
+        pre = mm(low[here, :], up[n]) + b_up[pl.ds(n, 1), :]
+        share = 0.5 + 0.5 * lax.erf(pre * (0.5**0.5))
+        slope[n, here, :] = share + pre * (jnp.exp(-0.5 * pre * pre) * 0.3989422804014327)
+        value = (pre * share).astype(BF16)
+        act[n, here, :] = value
+        fed[here, :] += mm(value, down[n])
+
+    @pl.loop(0, 2)
+    def _(r):
+        here = rows_of(r)
+        value, n2, r2 = norm_forward(fed[here, :], g2, s2)
+        layer_out[here, :] = value.astype(BF16)
+        cot = g[here, :].astype(F32)
+        scaled = cot * g2
+        grad_two = (
+            scaled
+            - jnp.mean(scaled, axis=-1, keepdims=True)
+            - n2 * jnp.mean(scaled * n2, axis=-1, keepdims=True)
+        ) * r2
+        add_to(3, grad_two)
+        add_to(4, cot * n2)
+        add_to(5, cot)
+        fed[here, :] = grad_two
+        d_fed[here, :] = grad_two.astype(BF16)
+        d_fed_t[:, here] = grad_two.T.astype(BF16)
+
+    def store(which, n):
+        src, dst = ((v_down, g_down), (v_up, g_up), (v_out, g_out))[which]
+        return pltpu.make_async_copy(src.at[n], dst.at[n], s_sem.at[which, n])
+
+    @pl.loop(0, parts)
+    def _(n):
+        v_down[n] = mm(d_fed_t[...], act[n]).astype(BF16)
+        store(0, n).start()
+
+        @pl.loop(0, 2)
+        def _(r):
+            here = rows_of(r)
+            grad = (mm_nt(d_fed[here, :], down[n]) * slope[n, here, :]).astype(BF16)
+            d_pre[here, :] = grad
+            sums[pl.ds(8 + n, 1), :] += jnp.sum(grad.astype(F32), axis=0, keepdims=True)
+            fed[here, :] += mm_nt(grad, up[n])
+
+        v_up[n] = mm(low_t[...], d_pre[...]).astype(BF16)
+        store(1, n).start()
+
+    @pl.loop(0, 2)
+    def _(r):
+        here = rows_of(r)
+        n1 = normed[here, :]
+        grad = fed[here, :]
+        scaled = grad * g1
+        value = (
+            scaled
+            - jnp.mean(scaled, axis=-1, keepdims=True)
+            - n1 * jnp.mean(scaled * n1, axis=-1, keepdims=True)
+        ) * inv[here, 0:1]
+        add_to(0, value)
+        add_to(1, grad * n1)
+        add_to(2, grad)
+        grad_one[here, :] = value
+        d_fed_t[:, here] = value.T.astype(BF16)
+        d_att = value.astype(BF16)
+        for n in range(parts):
+            d_ctx[n, here, :] = mm_nt(d_att, out[n]).astype(BF16)
+
+    @pl.loop(0, parts)
+    def _(n):
+        v_out[n] = mm(d_fed_t[...], ctx[n]).astype(BF16)
+        store(2, n).start()
+
+    for which in range(3):
+        for n in range(parts):
+            store(which, n).wait()
+
+
+def middle_part(parts, x_own, g_own, ctx_all, w_out, w_up, w_down, vecs, b_up):
     own, width = ctx_all.shape[1], ctx_all.shape[2]
     model = w_out.shape[2]
-    ctx = jnp.transpose(ctx_all, (1, 0, 2)).reshape(own, parts * width)
-    out_full = w_out.reshape(parts * width, model)
-    mixed_one = x_own + mm(ctx, out_full) + b_out
-    hidden_one, normed_one, spread_one = norm_forward(mixed_one, g1, s1)
-    low = hidden_one.astype(BF16)
-    pre = [mm(low, w_up[n]) + b_up[n] for n in range(parts)]
-    act = [gelu_exact(p).astype(BF16) for p in pre]
-    fed = sum(mm(act[n], w_down[n]) for n in range(parts))
-    mixed_two = hidden_one + fed + b_down
-    layer_out, normed_two, spread_two = norm_forward(mixed_two, g2, s2)
-    grad_two, gain_two, shift_two = norm_backward(g_own, normed_two, spread_two, g2)
-    d_fed = grad_two.astype(BF16)
-    grad_down = [mm_tn(d_fed, act[n]) for n in range(parts)]
-    d_pre = [jax.vjp(gelu_exact, pre[n])[1](mm_nt(d_fed, w_down[n]))[0].astype(BF16) for n in range(parts)]
-    grad_up = [mm_tn(low, d_pre[n]) for n in range(parts)]
-    up_bias = jnp.stack([jnp.sum(d.astype(F32), axis=0) for d in d_pre])
-    grad_hidden = grad_two + sum(mm_nt(d_pre[n], w_up[n]) for n in range(parts))
-    grad_one, gain_one, shift_one = norm_backward(grad_hidden, normed_one, spread_one, g1)
-    d_att = grad_one.astype(BF16)
-    grad_out = [mm_tn(d_att, ctx_all[n]) for n in range(parts)]
-    d_ctx = jnp.stack([mm_nt(d_att, w_out[n]).astype(BF16) for n in range(parts)])
-    small = jnp.stack(
-        [jnp.sum(grad_one, axis=0), gain_one, shift_one, jnp.sum(grad_two, axis=0), gain_two, shift_two]
-    )
-    return layer_out.astype(BF16), grad_one, d_ctx, grad_down, grad_up, grad_out, up_bias, small
+    units = w_up.shape[2]
+    vmem = pl.BlockSpec(memory_space=pltpu.VMEM)
+    hbm = pl.BlockSpec(memory_space=pl.ANY)
+    grads = [(parts, model, units), (parts, model, units), (parts, model, width)]
+    return pl.pallas_call(
+        functools.partial(middle_kernel, parts),
+        out_shape=[
+            jax.ShapeDtypeStruct((own, model), BF16),
+            jax.ShapeDtypeStruct((own, model), F32),
+            jax.ShapeDtypeStruct(ctx_all.shape, BF16),
+            jax.ShapeDtypeStruct((24, model), F32),
+        ]
+        + [jax.ShapeDtypeStruct(shape, BF16) for shape in grads],
+        in_specs=[vmem] * 5 + [hbm] * 3,
+        out_specs=[vmem] * 4 + [hbm] * 3,
+        scratch_shapes=[
+            pltpu.VMEM(w_out.shape, BF16),
+            pltpu.VMEM(w_up.shape, BF16),
+            pltpu.VMEM(w_down.shape, BF16),
+            pltpu.VMEM((parts, own, units), BF16),
+            pltpu.VMEM((parts, own, units), F32),
+            pltpu.VMEM((own, model), BF16),
+            pltpu.VMEM((model, own), BF16),
+            pltpu.VMEM((own, model), F32),
+            pltpu.VMEM((own, model), F32),
+            pltpu.VMEM((own, 128), F32),
+            pltpu.VMEM((own, model), F32),
+            pltpu.VMEM((own, model), BF16),
+            pltpu.VMEM((model, own), BF16),
+            pltpu.VMEM((own, units), BF16),
+        ]
+        + [pltpu.VMEM(shape, BF16) for shape in grads]
+        + [pltpu.SemaphoreType.DMA((3, parts))] * 2,
+        compiler_params=pltpu.CompilerParams(vmem_limit_bytes=60 * 1024 * 1024),
+        name="middle_part",
+    )(x_own, g_own, ctx_all, vecs, b_up, w_out, w_up, w_down)
 
 
 def per_device(
@@ -334,17 +879,41 @@
         jnp.pad(segment, (MOST, MOST), constant_values=-1)[:, None], (rows + 2 * MOST, 128)
     )
     bias = b_qv.astype(F32)[:, :, None]
-    q_t, k_n, v_t, lse, ctx_all, up_full, down_full, out_full = forward_part(
-        parts, tokens, w_qkv, bias, seg_row, seg_col, w_up, w_down, w_out
+    b_up_rows = jnp.broadcast_to(b_up.astype(F32)[None], (8, b_up.shape[0]))
+    q_t, k_n, v_t, lse, ctx_all, b_up_full, up_full, down_full, out_full = forward_part(
+        parts, tokens, w_qkv, bias, seg_row, seg_col, b_up_rows, w_up, w_down, w_out
     )
-    b_up_full = lax.all_gather(b_up, "tensor").astype(F32)
-    x_own = lax.dynamic_slice_in_dim(tokens, me * share, share, 0).astype(F32)
-    g_own = lax.dynamic_slice_in_dim(cotangent, me * share, share, 0).astype(F32)
-    layer_out, grad_one, d_ctx, grad_down, grad_up, grad_out, up_bias, small = middle_part(
-        parts, x_own, g_own, ctx_all, out_full, up_full, down_full,
-        b_out.astype(F32), ln1_gain.astype(F32), ln1_bias.astype(F32), b_up_full,
-        b_down.astype(F32), ln2_gain.astype(F32), ln2_bias.astype(F32),
+    x_own = lax.dynamic_slice_in_dim(tokens, me * share, share, 0)
+    g_own = lax.dynamic_slice_in_dim(cotangent, me * share, share, 0)
+    blank = jnp.zeros_like(b_out)
+    vecs = jnp.stack([b_out, ln1_gain, ln1_bias, b_down, ln2_gain, ln2_bias, blank, blank]).astype(F32)
+    layer_out, grad_one, d_ctx, sums, grad_down, grad_up, grad_out = middle_part(
+        parts, x_own, g_own, ctx_all, out_full, up_full, down_full, vecs, b_up_full
     )
+    if lax.axis_size("dp") == GROUP:
+        grads = [grad_down, grad_up, grad_out]
+        d_in, s_down, s_up, s_out, s_qkv, s_sums = backward_part(
+            parts, d_ctx, q_t, k_n, v_t, lse, seg_row, seg_col, tokens, w_qkv, grad_one, sums, grads
+        )
+        deep = sums.shape[1] // GROUP
+        own = lax.dynamic_slice_in_dim(s_sums, lax.axis_index("dp") * deep, deep, 1)
+        return (
+            layer_out,
+            d_in,
+            s_qkv,
+            s_sums[16:18, :width],
+            s_out.T,
+            own[0],
+            own[1],
+            own[2],
+            s_up,
+            lax.dynamic_index_in_dim(s_sums, 8 + me, 0, keepdims=False),
+            s_down.T,
+            own[3],
+            own[4],
+            own[5],
+        )
+    small, up_bias = sums[:6], sums[8 : 8 + parts]
     d_ctx_own = lax.all_to_all(d_ctx, "tensor", 0, 0).reshape(rows, width)
     dq, dk, dv = backward_plain(q_t, k_n, v_t, lse, d_ctx_own, segment)
     d_qkv = jnp.stack([dq, dk, dv])
@@ -361,8 +930,7 @@
     qkv_share = lax.psum_scatter(grad_qkv_t, "dp", scatter_dimension=0, tiled=True)
 
     def shared(blocks):
-        stacked = jnp.stack(blocks).astype(BF16)
-        over = lax.psum_scatter(stacked, "dp", scatter_dimension=1, tiled=True)
+        over = lax.psum_scatter(blocks, "dp", scatter_dimension=1, tiled=True)
         return lax.psum_scatter(over, "tensor", scatter_dimension=0, tiled=True)[0].astype(F32)
 
     return (

time: 557 us -> 274 us (0.49); the launches traced: 548 us -> 274 us
  Pallas kernels: 65.4 us -> 250 us
  matrix products: 183 us -> 0 us
  waiting for transfers between devices: 123 us -> 0 us
  other arithmetic: 72.9 us -> 0.89 us
  blocking collectives: 47 us -> 0 us
  between operations: 15.1 us -> 0.86 us
  local copies, waits for them, and re-layouts: 33.8 us -> 21.5 us
  starting transfers between devices: 7.88 us -> 0 us
    dot_general x40 -> x0, matrix products: 183 us -> none  [the longest x9 47.3 us: mm(): lax.dot_general(a, b, (((1,), (0,)), ((), ())), preferred_element_type=F32)]
    pallas_call x0 -> x2, Pallas kernels: none -> 182 us  [the longest x1 147 us: backward_part(): pl.pallas_call(functools.partial(backward_kernel, parts), out_shape=[jax....]
    reduce_scatter x6 -> x0, waiting for transfers between devices: 104 us -> none  [the longest x1 60.8 us: per_device(): lax.psum_scatter(partial_input.astype(BF16), 'tensor', scatter_dimension=...]
    convert_element_type x13 -> x1, other arithmetic: 51.3 us -> 0.61 us  [per_device(): jnp.stack([b_out, ln1_gain, ln1_bias, b_down, ln2_gain, ln2_bias, blank,...]
    unnamed x1 -> x0, blocking collectives: 19.4 us -> none
    unnamed x12 -> x0, waiting for transfers between devices: 19.2 us -> none
    all_gather x1 -> x0, blocking collectives: 14.8 us -> none  [per_device(): b_up_full = lax.all_gather(b_up, 'tensor').astype(F32)]
    unnamed x96 -> x30, local copies, waits for them, and re-layouts: 23 us -> 9.32 us
  transfers between devices with their start and end apart: 10 -> 0, of which waited for: 4 -> 0; matrix products, arithmetic and copies ran while one was open for 36% -> 0% of each run, Pallas kernels for 0% -> 0%
where the time goes in v2:
time: 274 us
  Pallas kernels  250 us (91%)
  local copies, waits for them, and re-layouts  21.5 us (8%)
    pallas_call x1, Pallas kernels, backward_part(): pl.pallas_call(functools.partial(backward_kernel, parts), out_shape=[jax....  147 us
    pallas_call x1, Pallas kernels, forward_part(): pl.pallas_call(functools.partial(forward_kernel, parts), out_shape=[jax.S...  68.4 us
    pallas_call x1, Pallas kernels, middle_part(): pl.pallas_call(functools.partial(middle_kernel, parts), out_shape=[jax.Sh...  35.1 us
    unnamed x30, local copies, waits for them, and re-layouts  9.32 us

profile of v2, /device:TPU:0, one launch (start us, length us, event | category | flops | bytes accessed | tf_op | source)
XLA Modules:
  0.0 273.7 jit_solution(6722878796551431731)
XLA Ops:
  0.6 0.0 copy-start.11
  0.7 0.0 copy-start
  0.7 0.0 copy-start.10
  0.7 0.0 copy-start.9
  0.7 2.7 constant_dynamic-slice_fusion.1
  3.4 0.0 copy-done.11
  3.4 0.2 reduce-window.8
  3.6 0.1 convert_reduce_fusion
  3.7 0.0 copy-start.2
  3.7 2.3 broadcast_in_dim.25.seg_col
  6.0 0.0 copy-done
  6.0 1.4 copy.38.wqkv
  7.4 0.0 copy-done.10
  7.4 0.8 copy.39.bias
  8.2 0.0 copy-done.9
  8.2 0.6 broadcast_in_dim.26.b_up
  8.8 0.0 copy-done.2
  8.8 0.0 copy-start.3
  8.8 0.0 copy-start.4
  8.8 0.0 copy-start.5
  8.9 0.0 copy-start.6
  8.9 0.0 copy-start.7
  8.9 0.0 copy-start.8
  8.9 68.4 %forward_part.1 = (bf16[192,2048]{1,0:T(8,128)(2,1)}, bf16[2048,192]{1,0:T(8,128)(2,1)}, bf16[192,2048]{1,0:T(8,128)(2,1)}, f32[3,2048]{1,0:T(4,128)}, bf16[4,51...) custom-call(bf16[2048,768]{1,0:T(8,128)(2,1)} %tok.3, ...), custom_call_target="tpu_custom_call" | custom-call | tf_op jit(solution)/shard_map/forward_part/pallas_call | solution.py:230
  77.3 0.9 copy.40
  78.2 0.6 slice_bitcast_fusion.b_up
  78.8 0.0 copy-done.3
  78.8 0.0 copy-done.4
  78.9 0.0 copy-done.5
  78.9 0.0 copy-done.6
  78.9 0.0 copy-done.7
  78.9 0.0 copy-done.8
  79.0 0.6 convert_element_type.12.vecs
  79.6 35.1 %middle_part.1 = (bf16[512,768]{1,0:T(8,128)(2,1)}, f32[512,768]{1,0:T(8,128)}, bf16[4,512,192]{2,1,0:T(8,128)(2,1)}, f32[24,768]{1,0:T(8,128)}, bf16[4,768,768]...) custom-call(bf16[512,768]{1,0:T(8,128)(2,1)} %get-tuple-element.107.x, ...), custom_call_target="tpu_custom_call" | custom-call | tf_op jit(solution)/shard_map/middle_part/pallas_call | solution.py:819
  114.8 146.9 %backward_part.1 = (bf16[512,768]{1,0:T(8,128)(2,1)}, f32[96,768]{1,0:T(8,128)}, f32[96,768]{1,0:T(8,128)}, f32[96,192]{1,0:T(8,128)}, f32[3,96,192]{2,1,0:T(8,128)}, /*index=5*/f32[24,768]{1,0:T(8,128)}) custom-call(bf16[4,512,192]{2,1,0:T(8,128)(2,1)} %get-tuple-element.42.d_ctx, bf16[192,2048]{1,0:T(8,128)(2,1)} %get-tuple-element.43.q_t, ...), custom_call_target="tpu_custom_call" | custom-call | tf_op jit(solution)/shard_map/backward_part/pallas_call | solution.py:620
  261.7 0.0 copy-start.1
  261.7 1.7 copy.42
  263.4 1.5 dynamic-slice_bitcast_fusion
  264.9 1.3 dynamic-slice_reduce_fusion
  266.2 1.3 slice.25
  267.5 2.1 copy.47
  269.6 1.7 copy.48
  271.3 1.7 copy.49
  272.9 0.0 copy-done.1
  272.9 0.7 copy.50
  (10 shorter events, 0.1 us)
Async XLA Ops:
  0.6 2.8 %copy-start.11 = (s32[1,8]{1,0:T(1,128)S(1)}, s32[1,8]{1,0:T(1,128)}, u32[]{:S(2)}) copy-start(s32[1,8]{1,0:T(1,128)} %param.16) | copy-start | bytes 100
  0.7 5.3 %copy-start = (bf16[3,768,192]{1,2,0:T(8,128)(2,1)S(1)}, bf16[3,768,192]{1,2,0:T(8,128)(2,1)}, u32[]{:S(2)}) copy-start(bf16[3,768,192]{1,2,0:T(8,128)(2,1)} %param.17) | copy-start | bytes 2654212
  0.7 6.7 %copy-start.10 = (bf16[2,192]{1,0:T(2,128)(2,1)S(1)}, bf16[2,192]{1,0:T(2,128)(2,1)}, u32[]{:S(2)}) copy-start(bf16[2,192]{1,0:T(2,128)(2,1)} %param.18) | copy-start | bytes 2308
  0.7 7.5 %copy-start.9 = (bf16[768]{0:T(1024)(128)(2,1)S(1)}, bf16[768]{0:T(1024)(128)(2,1)}, u32[]{:S(2)}) copy-start(bf16[768]{0:T(1024)(128)(2,1)} %param.24) | copy-start | bytes 4612
  3.7 5.2 %copy-start.2 = (s32[2048]{0:T(1024)}, s32[2048]{0:T(1024)S(1)}, u32[]{:S(2)}) copy-start(s32[2048]{0:T(1024)S(1)} %convert_reduce_fusion) | copy-start | bytes 24580
  8.8 70.0 %copy-start.3 = (bf16[768]{0:T(1024)(128)(2,1)S(1)}, bf16[768]{0:T(1024)(128)(2,1)}, u32[]{:S(2)}) copy-start(bf16[768]{0:T(1024)(128)(2,1)} %param.20) | copy-start | bytes 4612
  8.8 70.0 %copy-start.4 = (bf16[768]{0:T(1024)(128)(2,1)S(1)}, bf16[768]{0:T(1024)(128)(2,1)}, u32[]{:S(2)}) copy-start(bf16[768]{0:T(1024)(128)(2,1)} %param.21) | copy-start | bytes 4612
  8.8 70.0 %copy-start.5 = (bf16[768]{0:T(1024)(128)(2,1)S(1)}, bf16[768]{0:T(1024)(128)(2,1)}, u32[]{:S(2)}) copy-start(bf16[768]{0:T(1024)(128)(2,1)} %param.22) | copy-start | bytes 4612
  8.9 70.0 %copy-start.6 = (bf16[768]{0:T(1024)(128)(2,1)S(1)}, bf16[768]{0:T(1024)(128)(2,1)}, u32[]{:S(2)}) copy-start(bf16[768]{0:T(1024)(128)(2,1)} %param.26) | copy-start | bytes 4612
  8.9 70.0 %copy-start.7 = (bf16[768]{0:T(1024)(128)(2,1)S(1)}, bf16[768]{0:T(1024)(128)(2,1)}, u32[]{:S(2)}) copy-start(bf16[768]{0:T(1024)(128)(2,1)} %param.27) | copy-start | bytes 4612
  8.9 70.0 %copy-start.8 = (bf16[768]{0:T(1024)(128)(2,1)S(1)}, bf16[768]{0:T(1024)(128)(2,1)}, u32[]{:S(2)}) copy-start(bf16[768]{0:T(1024)(128)(2,1)} %param.28) | copy-start | bytes 4612
  261.7 11.3 %copy-start.1 = (f32[96,768]{1,0:T(8,128)S(1)}, f32[96,768]{1,0:T(8,128)}, u32[]{:S(2)}) copy-start(f32[96,768]{1,0:T(8,128)} %get-tuple-element.57) | copy-start | bytes 884740

commit v3 on v2

--- a/solution.py
+++ b/solution.py
@@ -56,12 +56,12 @@
 
 
 def forward_kernel(
-    parts, tok, wqkv, bias, seg_row, seg_col, b_up, up, down, out,
-    q_t, k_n, v_t, lse, ctx_all, b_all, up_all, down_all, out_all,
+    parts, tok, wqkv, bias, seg_row, ends, b_up, up, down, out,
+    q_t, k_n, v_t, lse, seg_col, ctx_all, b_all, up_all, down_all, out_all,
     k_pad, v_pad, ctx, z_send, z_recv, x_send, x_recv, c_send, c_recv, a_send, a_recv, b_send, b_recv, l_sem,
 ):
     rows = tok.shape[0]
-    width = wqkv.shape[2]
+    width = wqkv.shape[1]
     heads = width // HD
     share = rows // parts
     dp = lax.axis_index("dp")
@@ -139,16 +139,25 @@
         here = pl.ds(pl.multiple_of(t * TILE, TILE), TILE)
         there = pl.ds(pl.multiple_of(t * TILE + MOST, TILE), TILE)
         x = tok[here, :]
-        q_t[:, here] = (mm_tt(wqkv[0], x) + bias[0]).astype(BF16)
-        keys = mm(x, wqkv[1]).astype(BF16)
+        q_t[:, here] = (mm_nt(wqkv[0], x) + bias[0]).astype(BF16)
+        keys = mm_nt(x, wqkv[1]).astype(BF16)
         k_n[here, :] = keys
         for h in range(heads):
             k_pad[h, there, :] = keys[:, h * HD : (h + 1) * HD]
-        values = (mm_tt(wqkv[2], x) + bias[1]).astype(BF16)
+        values = (mm_nt(wqkv[2], x) + bias[1]).astype(BF16)
         v_t[:, here] = values
         v_pad[:, there] = values
 
     spread(0)
+
+    @pl.loop(0, (rows + 2 * MOST) // TILE)
+    def _(t):
+        spot = lax.broadcasted_iota(jnp.int32, (TILE, 128), 0) + (t * TILE - MOST)
+        number = jnp.zeros((TILE, 128), jnp.int32)
+        for i in range(ends.shape[0]):
+            number = number + (spot >= ends[i : i + 1, :]).astype(jnp.int32)
+        seg_col[pl.ds(pl.multiple_of(t * TILE, TILE), TILE), :] = jnp.where(spot < 0, -1, number)
+
     span = TILE + 2 * MOST
     per_block = share // TILE
     scale = HD ** (-0.5)
@@ -214,9 +223,9 @@
     keep.wait()
 
 
-def forward_part(parts, tokens, w_qkv, bias, seg_row, seg_col, b_up, w_up, w_down, w_out):
+def forward_part(parts, tokens, w_qkv, bias, seg_row, ends, b_up, w_up, w_down, w_out):
     rows, model = tokens.shape
-    width = w_qkv.shape[2]
+    width = w_qkv.shape[1]
     heads = width // HD
     share = rows // parts
 
@@ -234,12 +243,13 @@
             jax.ShapeDtypeStruct((rows, width), BF16),
             jax.ShapeDtypeStruct((width, rows), BF16),
             jax.ShapeDtypeStruct((heads, rows), F32),
+            jax.ShapeDtypeStruct((rows + 2 * MOST, 128), jnp.int32),
             jax.ShapeDtypeStruct((parts, share, width), BF16),
             jax.ShapeDtypeStruct((parts,) + b_up.shape, F32),
         ]
         + [jax.ShapeDtypeStruct((parts,) + s.shape, BF16) for s in shards],
         in_specs=[vmem] * 9,
-        out_specs=[vmem] * 6 + [hbm] * 3,
+        out_specs=[vmem] * 7 + [hbm] * 3,
         scratch_shapes=[
             pltpu.VMEM((heads, rows + 2 * MOST, HD), BF16),
             pltpu.VMEM((width, rows + 2 * MOST), BF16),
@@ -260,10 +270,10 @@
             collective_id=0, has_side_effects=True, vmem_limit_bytes=60 * 1024 * 1024
         ),
         name="forward_part",
-    )(tokens, w_qkv, bias, seg_row, seg_col, b_up, *shards)
-    q_t, k_n, v_t, lse, ctx_all, b_all, up_all, down_all, out_all = outs
+    )(tokens, w_qkv, bias, seg_row, ends, b_up, *shards)
+    q_t, k_n, v_t, lse, seg_col, ctx_all, b_all, up_all, down_all, out_all = outs
     return (
-        q_t, k_n, v_t, lse, ctx_all, b_all[:, 0],
+        q_t, k_n, v_t, lse, seg_col, ctx_all, b_all[:, 0],
         up_all.reshape((parts,) + w_up.shape),
         down_all.reshape((parts,) + w_down.shape),
         out_all.reshape((parts,) + w_out.shape),
@@ -271,16 +281,16 @@
 
 
 def backward_kernel(
-    parts, d_ctx, q_t, k_n, v_t, lse, seg_row, seg_col, tok, wqkv, g_own, sums, g_down, g_up, g_out,
+    parts, d_ctx, q_t, k_n, v_t, lse, seg_row, seg_col, tok, g_own, sums, w_hbm, g_down, g_up, g_out,
     d_in, s_down, s_up, s_out, s_qkv, s_sums,
-    dc, k_pad, v_pad, k_t, q_n, acc_k, acc_v, dq_t, dk, dv, part, chain,
-    p_down, p_up, p_out, r_down, r_up, r_out, x_down, x_up, x_out, z_down, z_up, z_out,
+    dc, k_pad, v_pad, k_t, q_n, acc_k, acc_v, pq, pk, rq, rk, w_all,
+    p_down, p_up, p_out, r_down, r_up, r_out, x_down, x_up, x_out, y_down, y_up, y_out, z_down, z_up, z_out,
     gq, r_gq, x_gq, sum_z, sum_dp, sum_in,
     a_send, a_recv, l_sem, s1_send, s1_recv, s2_send, s2_recv, s3_send, s3_recv,
-    h_send, h_recv, m_send, m_recv, n_send, n_recv,
+    e_send, e_recv, h_send, h_recv, m_send, m_recv, n_send, n_recv,
 ):
     rows, model = tok.shape
-    width = wqkv.shape[2]
+    width = q_t.shape[0]
     heads = width // HD
     share = rows // parts
     dp = lax.axis_index("dp")
@@ -289,11 +299,14 @@
     base = dp - rank
     core = rank % 2
     chip = rank // 2
+    along_y, along_x = chip // 2, chip % 2
     others = peers_of(rank)
+    starts = (2, 1, 2)
     full = (g_down, g_up, g_out)
     held = (p_down, p_up, p_out, gq)
     first = (r_down, r_up, r_out, r_gq)
-    second = (x_down, x_up, x_out, x_gq)
+    second = (x_down, x_up, x_out)
+    last = (y_down, y_up, y_out)
     third = (z_down, z_up, z_out)
     shared = (s_down, s_up, s_out)
     scale = HD ** (-0.5)
@@ -304,21 +317,44 @@
     fellows = [(rank + k) % GROUP for k in range(1, GROUP)]
     greet([(dp, at(j)) for j in range(1, parts)] + [(base + f, me) for f in fellows])
 
-    def a_copy(j):
-        return remote(d_ctx.at[at(j)], dc.at[me], a_send.at[j - 1], a_recv.at[j - 1], (dp, at(j)))
+    def order(k):
+        return jnp.where(me < parts // 2, (me + k) % parts, (me + parts - k) % parts)
+
+    def a_copy(to):
+        return remote(d_ctx.at[to], dc.at[me], a_send.at[to], a_recv.at[me], (dp, to))
+
+    def a_wait(source):
+        remote(d_ctx.at[source], dc.at[source], a_send.at[source], a_recv.at[source], (dp, source)).wait_recv()
 
     def s1_copy(w):
-        src = full[w].at[:, :, 1 - core] if w < 3 else gq.at[:, 1 - core]
+        src = full[w].at[:, :, :, 1 - core] if w < 3 else gq.at[:, 1 - core]
         return remote(src, first[w], s1_send.at[w], s1_recv.at[w], (base + others[0], me))
 
-    def s2_copy(w, k):
+    def s2_copy(w):
+        if starts[w] == 1:
+            src = held[w].at[:, :, 1 - along_x]
+        else:
+            src = held[w].at[:, 1 - along_y]
+        return remote(src, second[w], s2_send.at[w, 0], s2_recv.at[w, 0], (base + others[starts[w]], me))
+
+    def s2_then(w):
+        if starts[w] == 1:
+            src = held[w].at[:, 1 - along_y, along_x]
+        else:
+            src = held[w].at[:, along_y, 1 - along_x]
+        return remote(src, last[w], s2_send.at[w, 1], s2_recv.at[w, 1], (base + others[3 - starts[w]], me))
+
+    def gq_copy(k):
         to = others[1 + k]
-        src = held[w].at[:, to // 2] if w < 3 else gq.at[to // 2, core]
-        return remote(src, second[w].at[k], s2_send.at[w, k], s2_recv.at[w, k], (base + to, me))
+        return remote(gq.at[to // 2, core], x_gq.at[k], s2_send.at[3, k], s2_recv.at[3, k], (base + to, me))
 
     def s3_copy(w, j):
         return remote(
-            held[w].at[at(j), chip], third[w].at[j - 1], s3_send.at[w, j - 1], s3_recv.at[w, j - 1], (dp, at(j))
+            held[w].at[at(j), along_y, along_x],
+            third[w].at[j - 1],
+            s3_send.at[w, j - 1],
+            s3_recv.at[w, j - 1],
+            (dp, at(j)),
         )
 
     def m_copy(j):
@@ -327,16 +363,18 @@
     def n_copy(k):
         return remote(sum_in, sum_dp.at[k], n_send.at[k], n_recv.at[k], (base + fellows[k], me))
 
-    for j in range(1, parts):
-        a_copy(j).start()
+    for k in range(1, parts):
+        a_copy(order(k)).start()
     for j in range(1, parts):
         m_copy(j).start()
-    loads = [pltpu.make_async_copy(full[w].at[:, :, core], held[w], l_sem.at[w]) for w in range(3)]
+    loads = [pltpu.make_async_copy(full[w].at[:, :, :, core], held[w], l_sem.at[w]) for w in range(3)]
     for w in range(3):
         s1_copy(w).start()
         loads[w].start()
     mine = pltpu.make_async_copy(d_ctx.at[me], dc.at[me], l_sem.at[3])
     mine.start()
+    whole = pltpu.make_async_copy(w_hbm, w_all, l_sem.at[4])
+    whole.start()
 
     for ref in (k_pad, v_pad):
         ref[:MOST, :] = jnp.zeros((MOST, width), BF16)
@@ -367,21 +405,29 @@
         @pl.loop(0, parts)
         def _(n):
             for c in range(GROUP // 2):
-                held[w][n, c] = (held[w][n, c].astype(F32) + first[w][n, c].astype(F32)).astype(BF16)
-
-        for k in range(3):
-            s2_copy(w, k).start()
+                at_c = (n, c // 2, c % 2)
+                held[w][at_c] = (held[w][at_c].astype(F32) + first[w][at_c].astype(F32)).astype(BF16)
+
+        s2_copy(w).start()
 
     def s2_finish(w):
-        for k in range(3):
-            s2_copy(w, k).wait_recv()
+        s2_copy(w).wait_recv()
 
         @pl.loop(0, parts)
         def _(n):
-            total = held[w][n, chip].astype(F32)
-            for k in range(3):
-                total = total + second[w][k, n].astype(F32)
-            held[w][n, chip] = total.astype(BF16)
+            for c in range(2):
+                at_c = (n, c, along_x) if starts[w] == 1 else (n, along_y, c)
+                held[w][at_c] = (held[w][at_c].astype(F32) + second[w][n, c].astype(F32)).astype(BF16)
+
+        s2_then(w).start()
+
+    def s2_end(w):
+        s2_then(w).wait_recv()
+
+        @pl.loop(0, parts)
+        def _(n):
+            here = (n, along_y, along_x)
+            held[w][here] = (held[w][here].astype(F32) + last[w][n].astype(F32)).astype(BF16)
 
         for j in range(1, parts):
             s3_copy(w, j).start()
@@ -389,7 +435,7 @@
     def s3_finish(w):
         for j in range(1, parts):
             s3_copy(w, j).wait_recv()
-        total = held[w][me, chip].astype(F32)
+        total = held[w][me, along_y, along_x].astype(F32)
         for j in range(1, parts):
             total = total + third[w][j - 1].astype(F32)
         shared[w][...] = total
@@ -398,16 +444,7 @@
     per_block = share // TILE
     mine.wait()
 
-    @pl.loop(0, rows // TILE)
-    def _(step):
-        for j in range(1, parts):
-
-            @pl.when(step == j * per_block)
-            def _(j=j):
-                a_copy(parts - j).wait_recv()
-
-        block = (me + step // per_block) % parts
-        inner = (step % per_block) * TILE
+    def tile(block, inner):
         begin = block * share + inner
         here = pl.ds(pl.multiple_of(begin, TILE), TILE)
         window = pl.ds(pl.multiple_of(begin, TILE), span)
@@ -430,91 +467,81 @@
             inner_grad = (soft * (grad - shift)).astype(BF16)
             grads_v.append(mm(soft.astype(BF16), up_n[:, hs]))
             grads_k.append(mm(inner_grad, q_n[here, :][:, hs]))
-            dq_t[hs, here] = (mm(k_t[hs, window], inner_grad) * scale).astype(BF16)
+            grad_q = (mm(k_t[hs, window], inner_grad) * scale).astype(BF16)
+            pq[block, hs, pl.ds(pl.multiple_of(inner, TILE), TILE)] = grad_q
         acc_k[window, :] += jnp.concatenate(grads_k, axis=1)
         acc_v[window, :] += jnp.concatenate(grads_v, axis=1)
 
-        @pl.when(step == 1)
-        def _():
-            s1_finish(0)
-
-        @pl.when(step == 3)
-        def _():
-            s1_finish(1)
-
-        @pl.when(step == 4)
-        def _():
-            s1_finish(2)
-
-        @pl.when(step == 6)
-        def _():
-            s2_finish(0)
-
-    @pl.loop(0, rows // TILE)
-    def _(t):
-        here = pl.ds(pl.multiple_of(t * TILE, TILE), TILE)
-        there = pl.ds(pl.multiple_of(t * TILE + MOST, TILE), TILE)
-        dk[here, :] = acc_k[there, :].astype(BF16)
-        dv[here, :] = acc_v[there, :].astype(BF16)
-
-    def own_part(b):
+    def q_copy(b):
+        return remote(pq.at[b], rq.at[me], e_send.at[b], e_recv.at[me], (dp, b))
+
+    def k_copy(b):
+        return remote(pk.at[b], rk.at[me], h_send.at[b], h_recv.at[me], (dp, b))
+
+    def e_wait(m):
+        remote(pq.at[m], rq.at[m], e_send.at[m], e_recv.at[m], (dp, m)).wait_recv()
+        remote(pk.at[m], rk.at[m], h_send.at[m], h_recv.at[m], (dp, m)).wait_recv()
+
+    def finish(b):
         @pl.loop(0, per_block)
         def _(t):
-            here = pl.ds(pl.multiple_of(b * share + t * TILE, TILE), TILE)
-            total = mm_tt(dq_t[:, here], wqkv[0]) + mm_nt(dk[here, :], wqkv[1]) + mm_nt(dv[here, :], wqkv[2])
-            part[b, pl.ds(pl.multiple_of(t * TILE, TILE), TILE), :] = total.astype(BF16)
-
-    def right_copy(b):
-        return remote(part.at[b], chain.at[b], h_send.at[0, b], h_recv.at[0, b], (dp, me + 1))
-
-    def left_copy(b):
-        slot = jnp.where(b == me - 1, parts, b)
-        return remote(part.at[b], chain.at[slot], h_send.at[1, b], h_recv.at[1, b], (dp, me - 1))
-
-    def fold(b):
+            there = pl.ds(pl.multiple_of(b * share + t * TILE + MOST, TILE), TILE)
+            pair = jnp.concatenate([acc_k[there, :], acc_v[there, :]], axis=1)
+            pk[b, pl.ds(pl.multiple_of(t * TILE, TILE), TILE), :] = pair.astype(BF16)
+
+        @pl.when(b != me)
+        def _():
+            q_copy(b).start()
+            k_copy(b).start()
+
+    final = order(parts - 1)
+    s1_finish(0)
+    s1_finish(1)
+
+    @pl.loop(0, parts)
+    def _(k):
+        block = order(k)
+
+        @pl.when(k > 0)
+        def _():
+            a_wait(block)
+
         @pl.loop(0, per_block)
         def _(t):
-            here = pl.ds(pl.multiple_of(t * TILE, TILE), TILE)
-            part[b, here, :] = (part[b, here, :].astype(F32) + chain[b, here, :].astype(F32)).astype(BF16)
-
-    def go_right(b):
-        @pl.when(me < b)
+            tile(block, t * TILE)
+
+        for when, what, w in ((0, s1_finish, 2),):
+
+            @pl.when(k == when)
+            def _(what=what, w=w):
+                what(w)
+
+        @pl.when(k >= parts - 2)
         def _():
-            @pl.when(me > 0)
-            def _():
-                right_copy(b).wait_recv()
-                fold(b)
-
-            right_copy(b).start()
-
-    def go_left(b):
-        @pl.when(me > b)
-        def _():
-            @pl.when(me < parts - 1)
-            def _():
-                remote(part.at[b], chain.at[b], h_send.at[1, b], h_recv.at[1, b], (dp, me - 1)).wait_recv()
-                fold(b)
-
-            left_copy(b).start()
-
-    own_part(parts - 1)
-    own_part(0)
-    go_right(parts - 1)
-    go_left(0)
-    for b in range(parts - 2, 0, -1):
-        own_part(b)
-    s2_finish(1)
-
-    for c in range(3):
-        if c == 0:
-            grads = mm(dq_t[...], tok[...])
-        else:
-            grads = mm_tn((dk, dv)[c - 1][...], tok[...])
+            @pl.loop(0, parts)
+            def _(b):
+                early = (b - final >= 2) | (final - b >= 2)
+
+                @pl.when(early == (k == parts - 2))
+                def _():
+                    finish(b)
+
+    keep_q = pltpu.make_async_copy(pq.at[me], rq.at[me], l_sem.at[5])
+    keep_k = pltpu.make_async_copy(pk.at[me], rk.at[me], l_sem.at[6])
+    keep_q.start()
+    keep_k.start()
+    s2_finish(0)
+
+    deep = model // GROUP
+    rows_b = [slice(b * share, (b + 1) * share) for b in range(parts)]
+    grads_q = sum(mm(pq[b], tok[rows_b[b], :]) for b in range(parts))
+    grads_kv = sum(mm_tn(pk[b], tok[rows_b[b], :]) for b in range(parts))
+    for c, grads in enumerate((grads_q, grads_kv[:width], grads_kv[width:])):
         grads = grads.T.astype(BF16)
-        deep = model // GROUP
         for i in range(GROUP):
             gq[i // 2, i % 2, c] = grads[i * deep : (i + 1) * deep, :]
-    remote(gq.at[:, 1 - core], r_gq, s1_send.at[3], s1_recv.at[3], (base + others[0], me)).start()
+    s1_copy(3).start()
+    s2_finish(1)
     for j in range(1, parts):
         m_copy(j).wait_recv()
     total = sums[...]
@@ -522,29 +549,41 @@
         total = total + sum_z[j - 1]
     sum_in[...] = total
     keep = sum_in.shape[0] - 8
-    flat_q = jnp.sum(dq_t[...].astype(F32), axis=1, keepdims=True).T
-    flat_v = jnp.sum(dv[...].astype(F32), axis=0, keepdims=True)
+    flat_q = sum(jnp.sum(pq[b].astype(F32), axis=1, keepdims=True) for b in range(parts)).T
+    flat_v = sum(jnp.sum(pk[b].astype(F32), axis=0, keepdims=True) for b in range(parts))[:, width:]
     sum_in[keep : keep + 1, :width] = flat_q
     sum_in[keep + 1 : keep + 2, :width] = flat_v
     for k in range(GROUP - 1):
         n_copy(k).start()
 
-    go_right(parts - 2)
-    go_left(1)
     s1_copy(3).wait_recv()
     for c in range(GROUP // 2):
         for i in range(3):
             gq[c, core, i] = (gq[c, core, i].astype(F32) + r_gq[c, i].astype(F32)).astype(BF16)
+    s2_finish(2)
     for k in range(3):
-        s2_copy(3, k).start()
-    s2_finish(2)
-    for b in range(parts - 3, 0, -1):
-        go_right(b)
-    for b in range(2, parts - 1):
-        go_left(b)
+        gq_copy(k).start()
+    s2_end(0)
+    s2_end(1)
+    s2_end(2)
+    whole.wait()
+    keep_q.wait()
+    keep_k.wait()
+    for j in range(1, parts):
+        e_wait(at(j))
+
+    @pl.loop(0, per_block)
+    def _(t):
+        here = pl.ds(pl.multiple_of(t * TILE, TILE), TILE)
+        total = g_own[here, :]
+        for m in range(parts):
+            pair = rk[m, here, :]
+            total = total + mm_tn(rq[m, :, here], w_all[m, 0])
+            total = total + mm(pair[:, :width], w_all[m, 1]) + mm(pair[:, width:], w_all[m, 2])
+        d_in[here, :] = total.astype(BF16)
 
     for k in range(3):
-        s2_copy(3, k).wait_recv()
+        gq_copy(k).wait_recv()
     for i in range(3):
         block = gq[chip, core, i].astype(F32)
         for k in range(3):
@@ -559,56 +598,32 @@
     for w in range(3):
         s3_finish(w)
 
-    @pl.when(me > 0)
-    def _():
-        remote(part.at[me], chain.at[me], h_send.at[0, me], h_recv.at[0, me], (dp, me)).wait_recv()
-        fold(me)
-
-    @pl.when(me < parts - 1)
-    def _():
-        remote(part.at[me], chain.at[parts], h_send.at[1, me], h_recv.at[1, me], (dp, me)).wait_recv()
-
-        @pl.loop(0, per_block)
-        def _(t):
-            here = pl.ds(pl.multiple_of(t * TILE, TILE), TILE)
-            part[me, here, :] = (part[me, here, :].astype(F32) + chain[parts, here, :].astype(F32)).astype(BF16)
-
-    @pl.loop(0, per_block)
-    def _(t):
-        here = pl.ds(pl.multiple_of(t * TILE, TILE), TILE)
-        d_in[here, :] = (part[me, here, :].astype(F32) + g_own[here, :]).astype(BF16)
+    for k in range(1, parts):
+        a_copy(order(k)).wait_send()
+        q_copy(order(k)).wait_send()
+        k_copy(order(k)).wait_send()
 
     for j in range(1, parts):
-        a_copy(j).wait_send()
         m_copy(j).wait_send()
     for w in range(4):
         s1_copy(w).wait_send()
-        for k in range(3):
-            s2_copy(w, k).wait_send()
     for w in range(3):
+        gq_copy(w).wait_send()
+        s2_copy(w).wait_send()
+        s2_then(w).wait_send()
+    for w in range(3):
         for j in range(1, parts):
             s3_copy(w, j).wait_send()
-    for b in range(1, parts):
-
-        @pl.when(me < b)
-        def _(b=b):
-            right_copy(b).wait_send()
-
-    for b in range(parts - 1):
-
-        @pl.when(me > b)
-        def _(b=b):
-            left_copy(b).wait_send()
-
-
-def backward_part(parts, d_ctx, q_t, k_n, v_t, lse, seg_row, seg_col, tokens, w_qkv, g_own, sums, grads):
+
+
+def backward_part(parts, d_ctx, q_t, k_n, v_t, lse, seg_row, seg_col, tokens, qkv_full, g_own, sums, grads):
     rows, model = tokens.shape
-    width = w_qkv.shape[2]
+    width = q_t.shape[0]
     heads = width // HD
     share = rows // parts
     deep = model // GROUP
     wides = [g.shape[2] for g in grads]
-    blocks = [g.reshape(parts, GROUP // 2, 2, deep, g.shape[2]) for g in grads]
+    blocks = [g.reshape(parts, 2, 2, 2, deep, g.shape[2]) for g in grads]
     vmem = pl.BlockSpec(memory_space=pltpu.VMEM)
     hbm = pl.BlockSpec(memory_space=pl.ANY)
     dma = pltpu.SemaphoreType.DMA
@@ -622,7 +637,7 @@
         out_shape=[jax.ShapeDtypeStruct((share, model), BF16)]
         + [jax.ShapeDtypeStruct((deep, w), F32) for w in wides]
         + [jax.ShapeDtypeStruct((3, deep, width), F32), jax.ShapeDtypeStruct(sums.shape, F32)],
-        in_specs=[vmem] * 11 + [hbm] * 3,
+        in_specs=[vmem] * 10 + [hbm] * 4,
         out_specs=[vmem] * 6,
         scratch_shapes=[
             pltpu.VMEM((parts, share, width), BF16),
@@ -632,15 +647,16 @@
             pltpu.VMEM((rows, width), BF16),
             pltpu.VMEM((padded, width), F32),
             pltpu.VMEM((padded, width), F32),
-            pltpu.VMEM((width, rows), BF16),
-            pltpu.VMEM((rows, width), BF16),
-            pltpu.VMEM((rows, width), BF16),
-            pltpu.VMEM((parts, share, model), BF16),
-            pltpu.VMEM((parts + 1, share, model), BF16),
+            pltpu.VMEM((parts, width, share), BF16),
+            pltpu.VMEM((parts, share, 2 * width), BF16),
+            pltpu.VMEM((parts, width, share), BF16),
+            pltpu.VMEM((parts, share, 2 * width), BF16),
+            pltpu.VMEM(qkv_full.shape, BF16),
         ]
-        + held(parts, GROUP // 2)
-        + held(parts, GROUP // 2)
-        + held(3, parts)
+        + held(parts, 2, 2)
+        + held(parts, 2, 2)
+        + held(parts, 2)
+        + held(parts)
         + held(parts - 1)
         + [
             pltpu.VMEM((GROUP // 2, 2, 3, deep, width), BF16),
@@ -649,17 +665,19 @@
             pltpu.VMEM((parts - 1,) + sums.shape, F32),
             pltpu.VMEM((GROUP - 1,) + sums.shape, F32),
             pltpu.VMEM(sums.shape, F32),
-            dma((parts - 1,)),
-            dma((parts - 1,)),
-            dma((4,)),
+            dma((parts,)),
+            dma((parts,)),
+            dma((7,)),
             dma((4,)),
             dma((4,)),
             dma((4, 3)),
             dma((4, 3)),
             dma((3, parts - 1)),
             dma((3, parts - 1)),
-            dma((2, parts)),
-            dma((2, parts)),
+            dma((parts,)),
+            dma((parts,)),
+            dma((parts,)),
+            dma((parts,)),
             dma((parts - 1,)),
             dma((parts - 1,)),
             dma((GROUP - 1,)),
@@ -669,7 +687,7 @@
             collective_id=1, has_side_effects=True, vmem_limit_bytes=64 * 1024 * 1024 - 128 * 1024
         ),
         name="backward_part",
-    )(d_ctx, q_t, k_n, v_t, lse, seg_row, seg_col, tokens, w_qkv, g_own, sums, *blocks)
+    )(d_ctx, q_t, k_n, v_t, lse, seg_row, seg_col, tokens, g_own, sums, qkv_full, *blocks)
 
 
 def segment_ids(pair_lengths, count):
@@ -687,13 +705,18 @@
 
 
 def middle_kernel(
-    parts, x, g, ctx, vecs, b_up, out_hbm, up_hbm, down_hbm,
-    layer_out, grad_one, d_ctx, sums, g_down, g_up, g_out,
+    parts, ctx, vecs, b_up, wqkv, x_hbm, g_hbm, out_hbm, up_hbm, down_hbm,
+    layer_out, grad_one, d_ctx, sums, g_down, g_up, g_out, w_all,
     out, up, down, act, slope, low, low_t, hid, normed, inv, fed, d_fed, d_fed_t, d_pre,
-    v_down, v_up, v_out, l_sem, s_sem,
+    v_down, v_up, v_out, x, g, l_sem, s_sem, t_sem, z_send, z_recv, x_send, x_recv, c_send, c_recv, o_sem,
 ):
     own, model = x.shape
     half = own // 2
+    me = lax.axis_index("tensor")
+    mine = pl.ds(pl.multiple_of(me * own, own), own)
+    rows_in = [pltpu.make_async_copy(a.at[mine, :], b, t_sem.at[i]) for i, (a, b) in enumerate(((x_hbm, x), (g_hbm, g)))]
+    for copy in rows_in:
+        copy.start()
     loads = [
         pltpu.make_async_copy(a.at[n], b.at[n], l_sem.at[i, n])
         for i, (a, b) in enumerate(((out_hbm, out), (up_hbm, up), (down_hbm, down)))
@@ -701,9 +724,58 @@
     ]
     for load in loads:
         load.start()
+    dp = lax.axis_index("dp")
+    rank = dp % GROUP
+    base = dp - rank
+    others = peers_of(rank)
+
+    def at(j):
+        return (me + j) % parts
+
+    greet([(dp, at(j)) for j in range(1, parts)] + [(base + other, me) for other in others[:3]])
+
+    def z_copy(j):
+        return remote(
+            wqkv.at[:, rank], w_all.at[me, :, rank], z_send.at[j - 1], z_recv.at[j - 1], (dp, at(j))
+        )
+
+    def x_copy(j, k, slot, to):
+        piece = w_all.at[at(parts - j), :, slot]
+        return remote(piece, piece, x_send.at[j - 1, k], x_recv.at[j - 1, k], (base + to, me))
+
+    def c_copy(j, k, slot):
+        piece = w_all.at[at(parts - j), :, slot]
+        return remote(piece, piece, c_send.at[j - 1, k], c_recv.at[j - 1, k], (base + others[0], me))
+
+    for j in range(1, parts):
+        z_copy(j).start()
+    own_w = pltpu.make_async_copy(wqkv, w_all.at[me], o_sem)
+    own_w.start()
+
+    def spread():
+        for j in range(1, parts):
+            z_copy(j).wait_recv()
+            for k in (1, 2):
+                x_copy(j, k, rank, others[k]).start()
+
+    def relay():
+        for j in range(1, parts):
+            x_copy(j, 1, others[1], others[1]).wait_recv()
+            x_copy(j, 0, others[1], others[2]).start()
+            c_copy(j, 0, rank).start()
+            c_copy(j, 1, others[1]).start()
+
+    def pass_on():
+        for j in range(1, parts):
+            x_copy(j, 2, others[2], others[2]).wait_recv()
+            c_copy(j, 2, others[2]).start()
+        for j in range(1, parts):
+            x_copy(j, 0, others[3], others[2]).wait_recv()
+            c_copy(j, 3, others[3]).start()
+
     b_out, g1, s1, b_down, g2, s2 = [vecs[i : i + 1, :] for i in range(6)]
     sums[...] = jnp.zeros(sums.shape, F32)
-    for load in loads[:parts]:
+    for load in loads[:parts] + rows_in:
         load.wait()
 
     def rows_of(r):
@@ -739,6 +811,10 @@
         value = (pre * share).astype(BF16)
         act[n, here, :] = value
         fed[here, :] += mm(value, down[n])
+
+        @pl.when(t == 5)
+        def _():
+            spread()
 
     @pl.loop(0, 2)
     def _(r):
@@ -778,6 +854,10 @@
 
         v_up[n] = mm(low_t[...], d_pre[...]).astype(BF16)
         store(1, n).start()
+
+        @pl.when(n == 1)
+        def _():
+            relay()
 
     @pl.loop(0, 2)
     def _(r):
@@ -804,19 +884,30 @@
         v_out[n] = mm(d_fed_t[...], ctx[n]).astype(BF16)
         store(2, n).start()
 
+    pass_on()
     for which in range(3):
         for n in range(parts):
             store(which, n).wait()
-
-
-def middle_part(parts, x_own, g_own, ctx_all, w_out, w_up, w_down, vecs, b_up):
+    own_w.wait()
+    for j in range(1, parts):
+        z_copy(j).wait_send()
+        for k in (1, 2):
+            x_copy(j, k, rank, others[k]).wait_send()
+        x_copy(j, 0, others[3], others[2]).wait_send()
+        for k in range(4):
+            c_copy(j, k, others[0]).wait()
+
+
+def middle_part(parts, tokens, cotangent, ctx_all, w_out, w_up, w_down, vecs, b_up, w_qkv):
     own, width = ctx_all.shape[1], ctx_all.shape[2]
     model = w_out.shape[2]
     units = w_up.shape[2]
     vmem = pl.BlockSpec(memory_space=pltpu.VMEM)
     hbm = pl.BlockSpec(memory_space=pl.ANY)
     grads = [(parts, model, units), (parts, model, units), (parts, model, width)]
-    return pl.pallas_call(
+    pieces = w_qkv.reshape(3, GROUP, width // GROUP, model)
+    dma = pltpu.SemaphoreType.DMA
+    outs = pl.pallas_call(
         functools.partial(middle_kernel, parts),
         out_shape=[
             jax.ShapeDtypeStruct((own, model), BF16),
@@ -824,9 +915,10 @@
             jax.ShapeDtypeStruct(ctx_all.shape, BF16),
             jax.ShapeDtypeStruct((24, model), F32),
         ]
-        + [jax.ShapeDtypeStruct(shape, BF16) for shape in grads],
-        in_specs=[vmem] * 5 + [hbm] * 3,
-        out_specs=[vmem] * 4 + [hbm] * 3,
+        + [jax.ShapeDtypeStruct(shape, BF16) for shape in grads]
+        + [jax.ShapeDtypeStruct((parts,) + pieces.shape, BF16)],
+        in_specs=[vmem] * 4 + [hbm] * 5,
+        out_specs=[vmem] * 4 + [hbm] * 4,
         scratch_shapes=[
             pltpu.VMEM(w_out.shape, BF16),
             pltpu.VMEM(w_up.shape, BF16),
@@ -844,10 +936,19 @@
             pltpu.VMEM((own, units), BF16),
         ]
         + [pltpu.VMEM(shape, BF16) for shape in grads]
-        + [pltpu.SemaphoreType.DMA((3, parts))] * 2,
-        compiler_params=pltpu.CompilerParams(vmem_limit_bytes=60 * 1024 * 1024),
+        + [pltpu.VMEM((own, model), BF16)] * 2
+        + [dma((3, parts))] * 2
+        + [dma((2,))]
+        + [dma((parts - 1,))] * 2
+        + [dma((parts - 1, 3))] * 2
+        + [dma((parts - 1, 4))] * 2
+        + [dma],
+        compiler_params=pltpu.CompilerParams(
+            collective_id=2, has_side_effects=True, vmem_limit_bytes=62 * 1024 * 1024
+        ),
         name="middle_part",
-    )(x_own, g_own, ctx_all, vecs, b_up, w_out, w_up, w_down)
+    )(ctx_all, vecs, b_up, pieces, tokens, cotangent, w_out, w_up, w_down)
+    return (*outs[:-1], outs[-1].reshape((parts,) + w_qkv.shape))
 
 
 def per_device(
@@ -875,25 +976,22 @@
     me = lax.axis_index("tensor")
     segment = segment_ids(lengths[0], rows)
     seg_row = segment[None, :]
-    seg_col = jnp.broadcast_to(
-        jnp.pad(segment, (MOST, MOST), constant_values=-1)[:, None], (rows + 2 * MOST, 128)
-    )
+    ends = jnp.broadcast_to(jnp.cumsum(lengths[0])[:, None], (lengths.shape[1], 128))
+    w_rows = jnp.transpose(w_qkv, (0, 2, 1))
     bias = b_qv.astype(F32)[:, :, None]
     b_up_rows = jnp.broadcast_to(b_up.astype(F32)[None], (8, b_up.shape[0]))
-    q_t, k_n, v_t, lse, ctx_all, b_up_full, up_full, down_full, out_full = forward_part(
-        parts, tokens, w_qkv, bias, seg_row, seg_col, b_up_rows, w_up, w_down, w_out
+    q_t, k_n, v_t, lse, seg_col, ctx_all, b_up_full, up_full, down_full, out_full = forward_part(
+        parts, tokens, w_rows, bias, seg_row, ends, b_up_rows, w_up, w_down, w_out
     )
-    x_own = lax.dynamic_slice_in_dim(tokens, me * share, share, 0)
-    g_own = lax.dynamic_slice_in_dim(cotangent, me * share, share, 0)
     blank = jnp.zeros_like(b_out)
     vecs = jnp.stack([b_out, ln1_gain, ln1_bias, b_down, ln2_gain, ln2_bias, blank, blank]).astype(F32)
-    layer_out, grad_one, d_ctx, sums, grad_down, grad_up, grad_out = middle_part(
-        parts, x_own, g_own, ctx_all, out_full, up_full, down_full, vecs, b_up_full
+    layer_out, grad_one, d_ctx, sums, grad_down, grad_up, grad_out, qkv_full = middle_part(
+        parts, tokens, cotangent, ctx_all, out_full, up_full, down_full, vecs, b_up_full, w_rows
     )
     if lax.axis_size("dp") == GROUP:
         grads = [grad_down, grad_up, grad_out]
         d_in, s_down, s_up, s_out, s_qkv, s_sums = backward_part(
-            parts, d_ctx, q_t, k_n, v_t, lse, seg_row, seg_col, tokens, w_qkv, grad_one, sums, grads
+            parts, d_ctx, q_t, k_n, v_t, lse, seg_row, seg_col, tokens, qkv_full, grad_one, sums, grads
         )
         deep = sums.shape[1] // GROUP
         own = lax.dynamic_slice_in_dim(s_sums, lax.axis_index("dp") * deep, deep, 1)

time: 274 us -> 254 us (0.927)
  Pallas kernels: 250 us -> 234 us
  local copies, waits for them, and re-layouts: 21.5 us -> 16.5 us
    pallas_call x1, Pallas kernels: 147 us -> 120 us  [backward_part(): pl.pallas_call(functools.partial(backward_kernel, parts), out_shape=[jax....]
    pallas_call x1, Pallas kernels: 35.1 us -> 45.2 us  [middle_part(): pl.pallas_call(functools.partial(middle_kernel, parts), out_shape=[jax.Sh...]
    unnamed x30 -> x24, local copies, waits for them, and re-layouts: 9.32 us -> 8.01 us
where the time goes in v3:
time: 254 us
  Pallas kernels  234 us (92%)
  local copies, waits for them, and re-layouts  16.5 us (6%)
  other arithmetic  2.81 us (1%)
    pallas_call x1, Pallas kernels, backward_part(): pl.pallas_call(functools.partial(backward_kernel, parts), out_shape=[jax....  120 us
    pallas_call x1, Pallas kernels, forward_part(): pl.pallas_call(functools.partial(forward_kernel, parts), out_shape=[jax.S...  68.3 us
    pallas_call x1, Pallas kernels, middle_part(): pl.pallas_call(functools.partial(middle_kernel, parts), out_shape=[jax.Sh...  45.2 us
    unnamed x24, local copies, waits for them, and re-layouts  8.01 us

profile of v3, /device:TPU:0, one launch (start us, length us, event | category | flops | bytes accessed | tf_op | source)
XLA Modules:
  0.0 253.7 jit_solution(9773208182281783106)
XLA Ops:
  0.6 0.8 reduce-window.8
  1.5 0.7 convert_reduce_fusion
  2.2 0.7 broadcast_in_dim.25.ends
  2.8 0.7 bitcast_convert_fusion
  3.5 0.8 copy.34.bias
  4.3 1.3 broadcast_in_dim.26.b_up
  5.6 0.0 copy-start.3
  5.6 0.0 copy-start.4
  5.6 0.0 copy-start.5
  5.6 0.0 copy-start.6
  5.6 0.0 copy-start.7
  5.6 0.0 copy-start.8
  5.7 68.3 %forward_part.1 = (bf16[192,2048]{1,0:T(8,128)(2,1)}, bf16[2048,192]{1,0:T(8,128)(2,1)}, bf16[192,2048]{1,0:T(8,128)(2,1)}, f32[3,2048]{1,0:T(4,128)}, s32[3072,...) custom-call(bf16[2048,768]{1,0:T(8,128)(2,1)} %tok.3, ...), custom_call_target="tpu_custom_call" | custom-call | tf_op jit(solution)/shard_map/forward_part/pallas_call | solution.py:239
  74.0 0.9 copy.35
  74.9 0.6 slice_bitcast_fusion.b_up
  75.5 0.0 copy-done.3
  75.5 0.0 copy-done.4
  75.6 0.0 copy-done.5
  75.6 0.0 copy-done.6
  75.6 0.0 copy-done.7
  75.6 0.0 copy-done.8
  75.7 0.6 convert_element_type.12.vecs
  76.3 45.2 %middle_part.1 = (bf16[512,768]{1,0:T(8,128)(2,1)}, f32[512,768]{1,0:T(8,128)}, bf16[4,512,192]{2,1,0:T(8,128)(2,1)}, f32[24,768]{1,0:T(8,128)}, bf16[4,768,768]...) custom-call(bf16[4,512,192]{2,1,0:T(8,128)(2,1)} %get-tuple-element., ...), custom_call_target="tpu_custom_call" | custom-call | tf_op jit(solution)/shard_map/middle_part/pallas_call | solution.py:910
  121.5 120.0 %backward_part.1 = (bf16[512,768]{1,0:T(8,128)(2,1)}, f32[96,768]{1,0:T(8,128)}, f32[96,768]{1,0:T(8,128)}, f32[96,192]{1,0:T(8,128)}, f32[3,96,192]{2,1,0:T(8,128)}, /*index=5*/f32[24,768]{1,0:T(8,128)}) custom-call(bf16[4,512,192]{2,1,0:T(8,128)(2,1)} %get-tuple-element.44.d_ctx, bf16[192,2048]{1,0:T(8,128)(2,1)} %get-tuple-element.45.q_t, ...), custom_call_target="tpu_custom_call" | custom-call | tf_op jit(solution)/shard_map/backward_part/pallas_call | solution.py:635
  241.5 0.0 copy-start.2
  241.6 0.0 copy-start.1
  241.6 0.0 copy-start
  241.6 1.7 copy.36
  243.3 1.5 dynamic-slice_bitcast_fusion
  244.8 1.3 dynamic-slice_reduce_fusion
  246.2 1.3 slice.25
  247.4 2.1 copy.42
  249.5 2.1 copy.43
  251.6 0.0 copy-done.2
  251.6 0.7 copy.44
  252.3 0.0 copy-done.1
  252.3 0.7 copy.45
  253.0 0.0 copy-done
  253.0 0.7 copy.46
  (8 shorter events, 0.1 us)
Async XLA Ops:
  5.6 69.9 %copy-start.3 = (bf16[768]{0:T(1024)(128)(2,1)S(1)}, bf16[768]{0:T(1024)(128)(2,1)}, u32[]{:S(2)}) copy-start(bf16[768]{0:T(1024)(128)(2,1)} %param.20) | copy-start | bytes 4612
  5.6 69.9 %copy-start.4 = (bf16[768]{0:T(1024)(128)(2,1)S(1)}, bf16[768]{0:T(1024)(128)(2,1)}, u32[]{:S(2)}) copy-start(bf16[768]{0:T(1024)(128)(2,1)} %param.21) | copy-start | bytes 4612
  5.6 69.9 %copy-start.5 = (bf16[768]{0:T(1024)(128)(2,1)S(1)}, bf16[768]{0:T(1024)(128)(2,1)}, u32[]{:S(2)}) copy-start(bf16[768]{0:T(1024)(128)(2,1)} %param.22) | copy-start | bytes 4612
  5.6 70.0 %copy-start.6 = (bf16[768]{0:T(1024)(128)(2,1)S(1)}, bf16[768]{0:T(1024)(128)(2,1)}, u32[]{:S(2)}) copy-start(bf16[768]{0:T(1024)(128)(2,1)} %param.26) | copy-start | bytes 4612
  5.6 70.0 %copy-start.7 = (bf16[768]{0:T(1024)(128)(2,1)S(1)}, bf16[768]{0:T(1024)(128)(2,1)}, u32[]{:S(2)}) copy-start(bf16[768]{0:T(1024)(128)(2,1)} %param.27) | copy-start | bytes 4612
  5.6 70.0 %copy-start.8 = (bf16[768]{0:T(1024)(128)(2,1)S(1)}, bf16[768]{0:T(1024)(128)(2,1)}, u32[]{:S(2)}) copy-start(bf16[768]{0:T(1024)(128)(2,1)} %param.28) | copy-start | bytes 4612
  241.5 10.0 %copy-start.2 = (f32[3,96,192]{2,1,0:T(8,128)S(1)}, f32[3,96,192]{2,1,0:T(8,128)}, u32[]{:S(2)}) copy-start(f32[3,96,192]{2,1,0:T(8,128)} %get-tuple-element.126) | copy-start | bytes 663556
  241.6 10.7 %copy-start.1 = (f32[96,768]{1,0:T(8,128)S(1)}, f32[96,768]{1,0:T(8,128)}, u32[]{:S(2)}) copy-start(f32[96,768]{1,0:T(8,128)} %get-tuple-element.132) | copy-start | bytes 884740
  241.6 11.4 %copy-start = (f32[96,768]{1,0:T(8,128)S(1)}, f32[96,768]{1,0:T(8,128)}, u32[]{:S(2)}) copy-start(f32[96,768]{1,0:T(8,128)} %get-tuple-element.61) | copy-start | bytes 884740

commit v4 on v3

--- a/solution.py
+++ b/solution.py
@@ -106,28 +106,32 @@
     for copy in own:
         copy.start()
 
-    def spread(w):
-        for j in range(1, parts):
-            z_copy(w, j).wait_recv()
-            for k in (1, 2):
-                x_copy(w, j, k, rank, others[k]).start()
-
-    def relay(w):
+    def spread(w, j):
+        z_copy(w, j).wait_recv()
+        for k in (1, 2):
+            x_copy(w, j, k, rank, others[k]).start()
+
+    def relay(w, j):
         k = through[w]
-        for j in range(1, parts):
-            x_copy(w, j, k, others[k], others[k]).wait_recv()
-            x_copy(w, j, 0, others[k], others[3 - k]).start()
-            c_copy(w, j, 0, rank).start()
-            c_copy(w, j, k, others[k]).start()
-
-    def pass_on(w):
+        x_copy(w, j, k, others[k], others[k]).wait_recv()
+        x_copy(w, j, 0, others[k], others[3 - k]).start()
+        c_copy(w, j, 0, rank).start()
+        c_copy(w, j, k, others[k]).start()
+
+    def pass_on(w, j):
         k = 3 - through[w]
-        for j in range(1, parts):
-            x_copy(w, j, k, others[k], others[k]).wait_recv()
-            c_copy(w, j, k, others[k]).start()
-        for j in range(1, parts):
-            x_copy(w, j, 0, others[3], others[k]).wait_recv()
-            c_copy(w, j, 3, others[3]).start()
+        x_copy(w, j, k, others[k], others[k]).wait_recv()
+        c_copy(w, j, k, others[k]).start()
+        x_copy(w, j, 0, others[3], others[k]).wait_recv()
+        c_copy(w, j, 3, others[3]).start()
+
+    plan = (
+        [(0, spread, 1, 1), (1, spread, 1, 2), (2, spread, 1, 3), (4, spread, 2, 1), (5, spread, 2, 2), (6, spread, 2, 3)]
+        + [(1, relay, 0, j) for j in range(1, parts)]
+        + [(2, relay, 1, 1), (3, relay, 1, 2), (4, relay, 1, 3), (6, relay, 2, 1), (7, relay, 2, 2)]
+        + [(5, pass_on, 0, j) for j in range(1, parts)]
+        + [(6, pass_on, 1, 1), (7, pass_on, 1, 2)]
+    )
 
     k_pad[:, :MOST] = jnp.zeros((heads, MOST, HD), BF16)
     k_pad[:, MOST + rows :] = jnp.zeros((heads, MOST, HD), BF16)
@@ -148,7 +152,8 @@
         v_t[:, here] = values
         v_pad[:, there] = values
 
-    spread(0)
+    for j in range(1, parts):
+        spread(0, j)
 
     @pl.loop(0, (rows + 2 * MOST) // TILE)
     def _(t):
@@ -196,17 +201,20 @@
             def _(j=j):
                 a_copy(j).start()
 
-        for when, what, w in ((0, relay, 0), (1, spread, 1), (4, spread, 2), (5, relay, 1), (6, pass_on, 0)):
+        for when in range(8):
 
             @pl.when(step == when)
-            def _(what=what, w=w):
-                what(w)
+            def _(when=when):
+                for then, what, w, j in plan:
+                    if then == when:
+                        what(w, j)
 
     keep = pltpu.make_async_copy(ctx.at[me], ctx_all.at[me], l_sem.at[3])
     keep.start()
-    relay(2)
-    pass_on(1)
-    pass_on(2)
+    relay(2, 3)
+    pass_on(1, 3)
+    for j in range(1, parts):
+        pass_on(2, j)
     for j in range(1, parts):
         a_copy(j).wait()
         b_copy(j).wait()
@@ -495,9 +503,6 @@
             k_copy(b).start()
 
     final = order(parts - 1)
-    s1_finish(0)
-    s1_finish(1)
-
     @pl.loop(0, parts)
     def _(k):
         block = order(k)
@@ -510,7 +515,7 @@
         def _(t):
             tile(block, t * TILE)
 
-        for when, what, w in ((0, s1_finish, 2),):
+        for when, what, w in ((0, s1_finish, 0), (0, s1_finish, 1), (1, s1_finish, 2)):
 
             @pl.when(k == when)
             def _(what=what, w=w):
@@ -531,6 +536,7 @@
     keep_q.start()
     keep_k.start()
     s2_finish(0)
+    s2_finish(1)
 
     deep = model // GROUP
     rows_b = [slice(b * share, (b + 1) * share) for b in range(parts)]
@@ -541,7 +547,6 @@
         for i in range(GROUP):
             gq[i // 2, i % 2, c] = grads[i * deep : (i + 1) * deep, :]
     s1_copy(3).start()
-    s2_finish(1)
     for j in range(1, parts):
         m_copy(j).wait_recv()
     total = sums[...]

time: 254 us -> 249 us (0.980)
  Pallas kernels: 234 us -> 228 us
    pallas_call x1, Pallas kernels: 45.2 us -> 39.5 us  [middle_part(): pl.pallas_call(functools.partial(middle_kernel, parts), out_shape=[jax.Sh...]
where the time goes in v4:
time: 249 us
  Pallas kernels  228 us (92%)
  local copies, waits for them, and re-layouts  16.5 us (7%)
  other arithmetic  2.81 us (1%)
    pallas_call x1, Pallas kernels, backward_part(): pl.pallas_call(functools.partial(backward_kernel, parts), out_shape=[jax....  119 us
    pallas_call x1, Pallas kernels, forward_part(): pl.pallas_call(functools.partial(forward_kernel, parts), out_shape=[jax.S...  70.2 us
    pallas_call x1, Pallas kernels, middle_part(): pl.pallas_call(functools.partial(middle_kernel, parts), out_shape=[jax.Sh...  39.5 us
    unnamed x24, local copies, waits for them, and re-layouts  8.01 us

profile of v4, /device:TPU:0, one launch (start us, length us, event | category | flops | bytes accessed | tf_op | source)
XLA Modules:
  0.0 248.5 jit_solution(18387610161960962270)
XLA Ops:
  0.6 0.8 reduce-window.8
  1.5 0.7 convert_reduce_fusion
  2.2 0.7 broadcast_in_dim.25.ends
  2.8 0.7 bitcast_convert_fusion
  3.5 0.8 copy.34.bias
  4.3 1.3 broadcast_in_dim.26.b_up
  5.6 0.0 copy-start.3
  5.6 0.0 copy-start.4
  5.6 0.0 copy-start.5
  5.6 0.0 copy-start.6
  5.6 0.0 copy-start.7
  5.6 0.0 copy-start.8
  5.7 70.2 %forward_part.1 = (bf16[192,2048]{1,0:T(8,128)(2,1)}, bf16[2048,192]{1,0:T(8,128)(2,1)}, bf16[192,2048]{1,0:T(8,128)(2,1)}, f32[3,2048]{1,0:T(4,128)}, s32[3072,...) custom-call(bf16[2048,768]{1,0:T(8,128)(2,1)} %tok.3, ...), custom_call_target="tpu_custom_call" | custom-call | tf_op jit(solution)/shard_map/forward_part/pallas_call | solution.py:247
  75.8 0.9 copy.35
  76.8 0.6 slice_bitcast_fusion.b_up
  77.4 0.0 copy-done.3
  77.4 0.0 copy-done.4
  77.4 0.0 copy-done.5
  77.4 0.0 copy-done.6
  77.5 0.0 copy-done.7
  77.5 0.0 copy-done.8
  77.6 0.6 convert_element_type.12.vecs
  78.2 39.5 %middle_part.1 = (bf16[512,768]{1,0:T(8,128)(2,1)}, f32[512,768]{1,0:T(8,128)}, bf16[4,512,192]{2,1,0:T(8,128)(2,1)}, f32[24,768]{1,0:T(8,128)}, bf16[4,768,768]...) custom-call(bf16[4,512,192]{2,1,0:T(8,128)(2,1)} %get-tuple-element., ...), custom_call_target="tpu_custom_call" | custom-call | tf_op jit(solution)/shard_map/middle_part/pallas_call | solution.py:915
  117.6 118.7 %backward_part.1 = (bf16[512,768]{1,0:T(8,128)(2,1)}, f32[96,768]{1,0:T(8,128)}, f32[96,768]{1,0:T(8,128)}, f32[96,192]{1,0:T(8,128)}, f32[3,96,192]{2,1,0:T(8,128)}, /*index=5*/f32[24,768]{1,0:T(8,128)}) custom-call(bf16[4,512,192]{2,1,0:T(8,128)(2,1)} %get-tuple-element.44.d_ctx, bf16[192,2048]{1,0:T(8,128)(2,1)} %get-tuple-element.45.q_t, ...), custom_call_target="tpu_custom_call" | custom-call | tf_op jit(solution)/shard_map/backward_part/pallas_call | solution.py:640
  236.4 0.0 copy-start.2
  236.4 0.0 copy-start.1
  236.4 0.0 copy-start
  236.4 1.7 copy.36
  238.1 1.5 dynamic-slice_bitcast_fusion
  239.6 1.3 dynamic-slice_reduce_fusion
  241.0 1.3 slice.25
  242.2 2.1 copy.42
  244.3 2.1 copy.43
  246.4 0.0 copy-done.2
  246.4 0.7 copy.44
  247.1 0.0 copy-done.1
  247.1 0.7 copy.45
  247.8 0.0 copy-done
  247.8 0.7 copy.46
  (8 shorter events, 0.1 us)
Async XLA Ops:
  5.6 71.8 %copy-start.3 = (bf16[768]{0:T(1024)(128)(2,1)S(1)}, bf16[768]{0:T(1024)(128)(2,1)}, u32[]{:S(2)}) copy-start(bf16[768]{0:T(1024)(128)(2,1)} %param.20) | copy-start | bytes 4612
  5.6 71.8 %copy-start.4 = (bf16[768]{0:T(1024)(128)(2,1)S(1)}, bf16[768]{0:T(1024)(128)(2,1)}, u32[]{:S(2)}) copy-start(bf16[768]{0:T(1024)(128)(2,1)} %param.21) | copy-start | bytes 4612
  5.6 71.8 %copy-start.5 = (bf16[768]{0:T(1024)(128)(2,1)S(1)}, bf16[768]{0:T(1024)(128)(2,1)}, u32[]{:S(2)}) copy-start(bf16[768]{0:T(1024)(128)(2,1)} %param.22) | copy-start | bytes 4612
  5.6 71.8 %copy-start.6 = (bf16[768]{0:T(1024)(128)(2,1)S(1)}, bf16[768]{0:T(1024)(128)(2,1)}, u32[]{:S(2)}) copy-start(bf16[768]{0:T(1024)(128)(2,1)} %param.26) | copy-start | bytes 4612
  5.6 71.8 %copy-start.7 = (bf16[768]{0:T(1024)(128)(2,1)S(1)}, bf16[768]{0:T(1024)(128)(2,1)}, u32[]{:S(2)}) copy-start(bf16[768]{0:T(1024)(128)(2,1)} %param.27) | copy-start | bytes 4612
  5.6 71.8 %copy-start.8 = (bf16[768]{0:T(1024)(128)(2,1)S(1)}, bf16[768]{0:T(1024)(128)(2,1)}, u32[]{:S(2)}) copy-start(bf16[768]{0:T(1024)(128)(2,1)} %param.28) | copy-start | bytes 4612
  236.4 10.0 %copy-start.2 = (f32[3,96,192]{2,1,0:T(8,128)S(1)}, f32[3,96,192]{2,1,0:T(8,128)}, u32[]{:S(2)}) copy-start(f32[3,96,192]{2,1,0:T(8,128)} %get-tuple-element.126) | copy-start | bytes 663556
  236.4 10.7 %copy-start.1 = (f32[96,768]{1,0:T(8,128)S(1)}, f32[96,768]{1,0:T(8,128)}, u32[]{:S(2)}) copy-start(f32[96,768]{1,0:T(8,128)} %get-tuple-element.132) | copy-start | bytes 884740
  236.4 11.4 %copy-start = (f32[96,768]{1,0:T(8,128)S(1)}, f32[96,768]{1,0:T(8,128)}, u32[]{:S(2)}) copy-start(f32[96,768]{1,0:T(8,128)} %get-tuple-element.61) | copy-start | bytes 884740
